TPU v7x, 128 devices: a whole 4x4x4 slice. The times are simulated.
128 devices in a mesh: shard: 16 (over z, x), tensor: 8 (over y, core).
Axes of the slice: x: 4, y: 4, z: 4, core: 2. Of those that a mesh axis runs over, the one named last changes fastest.
Arguments:
- gradient: bfloat16 [768, 3072], P('shard', 'tensor'), may hold values from -12 to 12
- moment_one: float32 [768, 3072], P('shard', 'tensor'), may hold values from -6 to 6
- moment_two: float32 [768, 3072], P('shard', 'tensor'), may hold values from 0.5 to 8
- stat_left: float32 [768, 768], P('shard'), may hold values from -1 to 3, as said below
- stat_right: float32 [3072, 3072], P('shard', 'tensor'), may hold values from -1 to 3, as said below
- basis_left: float32 [768, 768], P('shard'), may hold values from -3 to 25, as said below
- basis_right: float32 [3072, 3072], P('shard', 'tensor'), may hold values from -3 to 47, as said below
Outputs:
- update: bfloat16 [768, 3072], P('shard', 'tensor')
- new_moment_one: float32 [768, 3072], P('shard', 'tensor')
- new_moment_two: float32 [768, 3072], P('shard', 'tensor')
- new_stat_left: float32 [768, 768], P('shard')
- new_stat_right: float32 [3072, 3072], P('shard', 'tensor')
- new_basis_left: float32 [768, 768], P('shard')
- new_basis_right: float32 [3072, 3072], P('shard', 'tensor')
Inputs may be any that keep to these rules, and one draw needn't show every extreme that they name: `stat_left`: symmetric and positive definite. `stat_right`: symmetric and positive definite. `basis_left`: full rank. `basis_right`: full rank.
All inputs are finite; a program needn't handle non-finite values.
Results may differ from a plain program's by a relative error of at most 0.011.
Values may be sent and summed in bfloat16 or wider, within the bound.
A program may use at most 64 MiB of HBM per device.

v0:
```python
import math

import jax
import jax.numpy as jnp
from jax import lax
from jax.sharding import PartitionSpec as P

D = 768
FF = 3072
NS_STEPS = 2


beta_one = 0.95
beta_two = 0.95
beta_stat = 0.95
correction = 1.0 - 0.95**10
adam_eps = 1e-08
highest = lax.Precision.HIGHEST


def blend_stat(previous, product, divisor):
    return beta_stat * previous + (1.0 - beta_stat) * (product / divisor)


def adam_moments(rotated, moment_one, moment_two):
    first_moment = beta_one * moment_one + (1.0 - beta_one) * rotated
    second_moment = beta_two * moment_two + (1.0 - beta_two) * (rotated * rotated)
    direction = (
        first_moment / correction / (jnp.sqrt(second_moment / correction) + adam_eps)
    ).astype(jnp.bfloat16)
    return (first_moment, second_moment, direction)


def local(gradient, moment_one, moment_two, stat_left, stat_right, basis_left, basis_right):
    rows_left = gradient.shape[0]
    rows_right = stat_right.shape[0]
    cols_right = stat_right.shape[1]
    shard_pos = lax.axis_index("shard")
    tensor_pos = lax.axis_index("tensor")
    row_start = shard_pos * rows_left
    grad_cols = lax.all_gather(gradient, "shard", axis=0, tiled=True)
    left_terms = jnp.dot(gradient, grad_cols.T, preferred_element_type=jnp.float32)
    gram_rows = lax.psum(left_terms.astype(jnp.bfloat16), "tensor").astype(jnp.float32)
    new_stat_left = blend_stat(stat_left, gram_rows, FF)
    grad_rows = lax.all_gather(gradient, "tensor", axis=1, tiled=True)
    gram_block = lax.psum_scatter(
        jnp.dot(grad_rows.T, gradient, preferred_element_type=jnp.float32).astype(jnp.bfloat16),
        "shard",
        scatter_dimension=0,
        tiled=True,
    ).astype(jnp.float32)
    new_stat_right = blend_stat(stat_right, gram_block, D)
    basis_all = lax.all_gather(basis_left, "shard", axis=0, tiled=True)
    left_q_all = basis_all / math.sqrt(D)
    left_qb_all = left_q_all.astype(jnp.bfloat16)
    left_qb_own = lax.dynamic_slice_in_dim(left_qb_all, row_start, rows_left, 0)
    left_cols_own = lax.dynamic_slice_in_dim(left_qb_all, row_start, rows_left, 1)
    half_rotated = jnp.dot(left_cols_own.T, grad_cols, preferred_element_type=jnp.float32).astype(
        jnp.bfloat16
    )
    right_q = basis_right / math.sqrt(FF)
    right_qb = right_q.astype(jnp.bfloat16)
    right_cols_b = lax.all_gather(right_qb, "shard", axis=0, tiled=True)
    half_full = lax.all_gather(half_rotated, "tensor", axis=1, tiled=True)
    rotated = jnp.dot(half_full, right_cols_b, preferred_element_type=jnp.float32)
    new_moment_one, new_moment_two, direction = adam_moments(rotated, moment_one, moment_two)
    back_half = jnp.dot(
        left_qb_own,
        lax.all_gather(direction, "shard", axis=0, tiled=True),
        preferred_element_type=jnp.float32,
    ).astype(jnp.bfloat16)
    back_terms = jnp.dot(back_half, right_cols_b.T, preferred_element_type=jnp.float32)
    update = lax.psum_scatter(back_terms, "tensor", scatter_dimension=1, tiled=True).astype(
        jnp.bfloat16
    )
    stat_rows = lax.all_gather(new_stat_right, "tensor", axis=1, tiled=True)
    power_right = jnp.dot(
        stat_rows,
        lax.all_gather(right_q, "shard", axis=0, tiled=True),
        precision=highest,
        preferred_element_type=jnp.float32,
    )
    power_left = jnp.dot(
        new_stat_left, left_q_all, precision=highest, preferred_element_type=jnp.float32
    )
    local_left = jnp.sum(power_left * power_left)
    local_right = jnp.sum(power_right * power_right)
    total_left = lax.psum(local_left, "shard")
    total_right = lax.psum(local_right, ("shard", "tensor"))
    iterate_left = power_left * (math.sqrt(D) / (4.0 * jnp.sqrt(total_left)))
    for iteration in range(NS_STEPS):
        partial_gram = jnp.dot(
            iterate_left.T, iterate_left, precision=highest, preferred_element_type=jnp.float32
        )
        gram_left = lax.psum(partial_gram.astype(jnp.bfloat16), "shard").astype(jnp.float32)
        iterate_left = 1.5 * iterate_left - 0.5 * jnp.dot(
            iterate_left, gram_left, precision=highest, preferred_element_type=jnp.float32
        )
    iterate_right = power_right * (math.sqrt(FF) / (4.0 * jnp.sqrt(total_right)))
    row_ids = shard_pos * rows_right + lax.broadcasted_iota(jnp.int32, (rows_right, cols_right), 0)
    col_ids = tensor_pos * cols_right + lax.broadcasted_iota(jnp.int32, (rows_right, cols_right), 1)
    identity_tile = (row_ids == col_ids).astype(jnp.float32)
    for iteration in range(NS_STEPS):
        rounded_iterate = iterate_right.astype(jnp.bfloat16)
        iterate_rows = lax.all_gather(rounded_iterate, "tensor", axis=1, tiled=True)
        gram_right = lax.psum_scatter(
            jnp.dot(iterate_rows.T, rounded_iterate, preferred_element_type=jnp.float32).astype(
                jnp.bfloat16
            ),
            "shard",
            scatter_dimension=0,
            tiled=True,
        ).astype(jnp.float32)
        mixing = (1.5 * identity_tile - 0.5 * gram_right).astype(jnp.bfloat16)
        iterate_right = jnp.dot(
            iterate_rows,
            lax.all_gather(mixing, "shard", axis=0, tiled=True),
            preferred_element_type=jnp.float32,
        )
    return (
        update,
        new_moment_one,
        new_moment_two,
        new_stat_left,
        new_stat_right,
        iterate_left * math.sqrt(D),
        iterate_right * math.sqrt(FF),
    )


def solution(mesh):
    placed = (
        P("shard", "tensor"),
        P("shard", "tensor"),
        P("shard", "tensor"),
        P("shard", None),
        P("shard", "tensor"),
        P("shard", None),
        P("shard", "tensor"),
    )
    return jax.shard_map(
        local,
        mesh=mesh,
        in_specs=placed,
        out_specs=(
            P("shard", "tensor"),
            P("shard", "tensor"),
            P("shard", "tensor"),
            P("shard", None),
            P("shard", "tensor"),
            P("shard", None),
            P("shard", "tensor"),
        ),
        check_vma=False,
    )
```

profile of v0, /device:TPU:0, one launch (start us, length us, event | category | flops | bytes accessed | tf_op | source)
XLA Modules:
  0.0 935.4 jit_solution(6653130991982937467)
XLA Ops:
  7.2 13.8 %all_gather.41 = bf16[48,3072]{1,0:T(8,128)(2,1)S(1)} all-gather(bf16[48,384]{1,0:T(8,128)(2,1)} %param.7), channel_id=1, replica_groups=mesh['shard'=16,'tensor'=8] {'tensor'}, dimensions={1}, use_global_device_ids=true | all-gather | bytes 331776 | tf_op jit(solution)/shard_map/all_gather | solution.py:45
  21.0 3.1 convolution_convert_fusion.2
  24.1 77.6 %reduce-scatter.7.cloned.1.call-done = bf16[192,384]{1,0:T(8,128)(2,1)} async-done(((bf16[3072,384]{1,0:T(8,128)(2,1)}), bf16[192,384]{1,0:T(8,128)(2,1)}) %reduce-scatter.7.cloned.1.call-update) | async-done | bytes 147472 | tf_op jit(solution)/shard_map/reduce_scatter | solution.py:46
  104.4 24.5 %all-gather.13.cloned.1.call-done = f32[192,3072]{1,0:T(8,128)} async-done(((f32[192,384]{1,0:T(8,128)}), f32[192,3072]{1,0:T(8,128)}) %all-gather.13.cloned.1.call-update) | async-done | bytes 2359312 | tf_op jit(solution)/shard_map/all_gather | solution.py:76
  128.9 57.2 %all-gather.15.cloned.1.call-done = f32[3072,384]{1,0:T(8,128)} async-done(((f32[192,384]{1,0:T(8,128)}), f32[3072,384]{1,0:T(8,128)}) %all-gather.15.cloned.1.call-update) | async-done | bytes 4718608 | tf_op jit(solution)/shard_map/all_gather | solution.py:79
  186.1 7.8 multiply_reduce_fusion
  193.9 64.5 %psum.39 = f32[]{:T(128)} all-reduce(f32[]{:T(128)} %get-tuple-element.14), channel_id=1, replica_groups=mesh['shard'=16,'tensor'=8] {'shard','tensor'}, use_global_device_ids=true, to_apply=%region_8.0 | all-reduce | flops 1 | bytes 8 | tf_op jit(solution)/shard_map/psum | solution.py:89
  259.9 21.0 %all-gather.17.cloned.1.call-done = bf16[192,3072]{1,0:T(8,128)(2,1)} async-done(((bf16[192,384]{1,0:T(8,128)(2,1)}), bf16[192,3072]{1,0:T(8,128)(2,1)}) %all-gather.17.cloned.1.call-update) | async-done | bytes 1179664 | tf_op jit(solution)/shard_map/all_gather | solution.py:105
  280.9 3.7 convolution_convert_fusion.1
  284.7 75.9 %reduce-scatter.9.cloned.1.call-done = bf16[192,384]{1,0:T(8,128)(2,1)} async-done(((bf16[3072,384]{1,0:T(8,128)(2,1)}), bf16[192,384]{1,0:T(8,128)(2,1)}) %reduce-scatter.9.cloned.1.call-update) | async-done | bytes 147472 | tf_op jit(solution)/shard_map/reduce_scatter | solution.py:106
  362.3 23.6 %all_gather.37 = bf16[768,384]{1,0:T(8,128)(2,1)S(1)} all-gather(bf16[48,384]{1,0:T(8,128)(2,1)S(1)} %copy-done.7), channel_id=1, replica_groups=mesh['shard'=16,'tensor'=8] {'shard'}, dimensions={0}, use_global_device_ids=true | all-gather | bytes 626688 | tf_op jit(solution)/shard_map/all_gather | solution.py:41
  387.7 21.1 %all-gather.19.cloned.1.call-done = bf16[3072,384]{1,0:T(8,128)(2,1)} async-done(((bf16[192,384]{1,0:T(8,128)(2,1)}), bf16[3072,384]{1,0:T(8,128)(2,1)}) %all-gather.19.cloned.1.call-update) | async-done | bytes 2359312 | tf_op jit(solution)/shard_map/all_gather | solution.py:117
  408.7 3.1 convolution_convert_fusion.5
  412.5 53.3 %all-reduce.4.cloned.1.call-done = bf16[48,768]{1,0:T(8,128)(2,1)} async-done(((bf16[48,768]{1,0:T(8,128)(2,1)}), bf16[48,768]{1,0:T(8,128)(2,1)}) %all-reduce.4.cloned.1.call-update) | async-done | bytes 73744 | tf_op jit(solution)/shard_map/psum | solution.py:43
  466.8 47.2 %all-gather.9.cloned.1.call-done = f32[768,768]{1,0:T(8,128)} async-done(((f32[48,768]{1,0:T(8,128)}), f32[768,768]{1,0:T(8,128)}) %all-gather.9.cloned.1.call-update) | async-done | bytes 2359312 | tf_op jit(solution)/shard_map/all_gather | solution.py:53
  513.9 3.8 multiply_reduce_fusion.1
  517.7 39.0 %psum.36 = f32[]{:T(128)} all-reduce(f32[]{:T(128)} %get-tuple-element.12), channel_id=1, replica_groups=mesh['shard'=16,'tensor'=8] {'shard'}, use_global_device_ids=true, to_apply=%region_4.0 | all-reduce | flops 1 | bytes 8 | tf_op jit(solution)/shard_map/psum | solution.py:88
  557.5 3.1 convolution_convert_fusion.4
  560.7 3.9 convolution_convert_fusion
  565.9 13.2 %all_gather.38 = bf16[48,3072]{1,0:T(8,128)(2,1)S(1)} all-gather(bf16[48,384]{1,0:T(8,128)(2,1)S(1)} %convolution_convert_fusion.8), channel_id=1, replica_groups=mesh['shard'=16,'tensor'=8] {'tensor'}, dimensions={1}, use_global_device_ids=true | all-gather | bytes 331776 | tf_op jit(solution)/shard_map/all_gather | solution.py:64
  579.2 8.1 all-gather.11.cloned.1.call-done
  587.3 3.0 divide_convert_fusion
  590.2 24.4 %all_gather.40 = bf16[768,384]{1,0:T(8,128)(2,1)S(1)} all-gather(bf16[48,384]{1,0:T(8,128)(2,1)S(1)} %get-tuple-element.7), channel_id=1, replica_groups=mesh['shard'=16,'tensor'=8] {'shard'}, dimensions={0}, use_global_device_ids=true | all-gather | bytes 626688 | tf_op jit(solution)/shard_map/all_gather | solution.py:69
  614.6 2.7 fusion.6
  617.4 60.1 %all-reduce.6.cloned.1.call-done = bf16[768,768]{1,0:T(8,128)(2,1)} async-done(((bf16[768,768]{1,0:T(8,128)(2,1)}), bf16[768,768]{1,0:T(8,128)(2,1)}) %all-reduce.6.cloned.1.call-update) | async-done | bytes 1179664 | tf_op jit(solution)/shard_map/psum | solution.py:95
  679.4 3.1 convolution_convert_fusion.3
  682.6 73.2 %reduce-scatter.11.cloned.1.call-done = bf16[192,384]{1,0:T(8,128)(2,1)} async-done(((bf16[3072,384]{1,0:T(8,128)(2,1)}), bf16[192,384]{1,0:T(8,128)(2,1)}) %reduce-scatter.11.cloned.1.call-update) | async-done | bytes 147472 | tf_op jit(solution)/shard_map/reduce_scatter | solution.py:106
  757.5 31.4 %reduce-scatter.5.cloned.1.call-done = f32[48,384]{1,0:T(8,128)} async-done(((f32[48,3072]{1,0:T(8,128)}), f32[48,384]{1,0:T(8,128)}) %reduce-scatter.5.cloned.1.call-update) | async-done | bytes 73744 | tf_op jit(solution)/shard_map/reduce_scatter | solution.py:73
  790.5 87.6 %all-reduce.8.cloned.1.call-done = bf16[768,768]{1,0:T(8,128)(2,1)} async-done(((bf16[768,768]{1,0:T(8,128)(2,1)}), bf16[768,768]{1,0:T(8,128)(2,1)}) %all-reduce.8.cloned.1.call-update) | async-done | bytes 1179664 | tf_op jit(solution)/shard_map/psum | solution.py:95
  878.1 2.6 fusion.4
  880.7 45.0 %all-gather.23.cloned.1.call-done = bf16[3072,384]{1,0:T(8,128)(2,1)} async-done(((bf16[192,384]{1,0:T(8,128)(2,1)}), bf16[3072,384]{1,0:T(8,128)(2,1)}) %all-gather.23.cloned.1.call-update) | async-done | bytes 2359312 | tf_op jit(solution)/shard_map/all_gather | solution.py:117
  925.7 3.2 convolution_multiply_fusion
  (70 shorter events, 15.2 us)
Async XLA Ops:
  7.2 94.6 %reduce-scatter.7.cloned.1.call-start = ((), (), s32[]{:S(2)}) async-start(), calls=%async_computation.8 | async-start | bytes 2506752 | tf_op jit(solution)/shard_map/reduce_scatter | solution.py:46
  21.0 80.8 %copy-start.8 = (f32[192,384]{1,0:T(8,128)S(1)}, f32[192,384]{1,0:T(8,128)}, u32[]{:S(2)}) copy-start(f32[192,384]{1,0:T(8,128)} %param.11) | copy-start | bytes 884740
  24.1 79.5 %copy-start.9 = (f32[192,384]{1,0:T(8,128)S(1)}, f32[192,384]{1,0:T(8,128)}, u32[]{:S(2)}) copy-start(f32[192,384]{1,0:T(8,128)} %param.13) | copy-start | bytes 884740
  24.1 104.8 %all-gather.13.cloned.1.call-start = ((), (), s32[]{:S(2)}) async-start(), calls=%async_computation.11 | async-start | bytes 2654208 | tf_op jit(solution)/shard_map/all_gather | solution.py:76
  103.5 82.6 %all-gather.15.cloned.1.call-start = ((), (), s32[]{:S(2)}) async-start(), calls=%async_computation.12 | async-start | bytes 5013504 | tf_op jit(solution)/shard_map/all_gather | solution.py:79
  104.4 176.5 %all-gather.17.cloned.1.call-start = ((), (), s32[]{:S(2)}) async-start(), calls=%async_computation.13 | async-start | bytes 1327104 | tf_op jit(solution)/shard_map/all_gather | solution.py:105
  259.8 102.5 %copy-start.7 = (bf16[48,384]{1,0:T(8,128)(2,1)S(1)}, bf16[48,384]{1,0:T(8,128)(2,1)}, u32[]{:S(2)}) copy-start(bf16[48,384]{1,0:T(8,128)(2,1)} %param.7) | copy-start | bytes 110596
  259.8 100.7 %reduce-scatter.9.cloned.1.call-start = ((), (), s32[]{:S(2)}) async-start(), calls=%async_computation.14 | async-start | bytes 2506752 | tf_op jit(solution)/shard_map/reduce_scatter | solution.py:106
  284.6 124.2 %copy-start.4 = (bf16[192,3072]{1,0:T(8,128)(2,1)S(1)}, bf16[192,3072]{1,0:T(8,128)(2,1)}, u32[]{:S(2)}) copy-start(bf16[192,3072]{1,0:T(8,128)(2,1)} %all-gather.17.cloned.1.call-done) | copy-start | bytes 3538948
  284.6 124.1 %all-gather.19.cloned.1.call-start = ((), (), s32[]{:S(2)}) async-start(), calls=%async_computation.15 | async-start | bytes 2506752 | tf_op jit(solution)/shard_map/all_gather | solution.py:117
  362.3 103.5 %all-reduce.4.cloned.1.call-start = ((), (), s32[]{:S(2)}) async-start(), calls=%async_computation.7 | async-start | bytes 147456 | tf_op jit(solution)/shard_map/psum | solution.py:43
  386.9 127.0 %all-gather.9.cloned.1.call-start = ((), (), s32[]{:S(2)}) async-start(), calls=%async_computation.4 | async-start | bytes 2506752 | tf_op jit(solution)/shard_map/all_gather | solution.py:53
  387.6 78.2 %copy-start.10 = (f32[48,768]{1,0:T(8,128)S(1)}, f32[48,768]{1,0:T(8,128)}, u32[]{:S(2)}) copy-start(f32[48,768]{1,0:T(8,128)} %param.10) | copy-start | bytes 442372
  387.6 173.0 %all-gather.21.cloned.1.call-start = ((), (), s32[]{:S(2)}) async-start(), calls=%async_computation.16 | async-start | bytes 1327104 | tf_op jit(solution)/shard_map/all_gather | solution.py:105
  411.9 175.4 %all-gather.11.cloned.1.call-start = ((), (), s32[]{:S(2)}) async-start(), calls=%async_computation.5 | async-start | bytes 2506752 | tf_op jit(solution)/shard_map/all_gather | solution.py:63
  412.5 264.9 %all-reduce.6.cloned.1.call-start = ((), (), s32[]{:S(2)}) async-start(), calls=%async_computation.9 | async-start | bytes 2359296 | tf_op jit(solution)/shard_map/psum | solution.py:95
  466.7 93.9 %copy-start.6 = (f32[48,768]{1,0:T(8,128)}, f32[48,768]{1,0:T(8,128)S(1)}, u32[]{:S(2)}) copy-start(f32[48,768]{1,0:T(8,128)S(1)} %multiply_add_fusion.1) | copy-start | bytes 442372
  466.7 93.9 %copy-start.5 = (bf16[192,384]{1,0:T(8,128)(2,1)S(1)}, bf16[192,384]{1,0:T(8,128)(2,1)}, u32[]{:S(2)}) copy-start(bf16[192,384]{1,0:T(8,128)(2,1)} %convolution_convert_fusion.5) | copy-start | bytes 442372
  560.6 4.1 copy-start
  560.6 195.2 %reduce-scatter.11.cloned.1.call-start = ((), (), s32[]{:S(2)}) async-start(), calls=%async_computation.17 | async-start | bytes 2506752 | tf_op jit(solution)/shard_map/reduce_scatter | solution.py:106
  564.6 22.6 %copy-start.11 = (f32[48,384]{1,0:T(8,128)S(1)}, f32[48,384]{1,0:T(8,128)}, u32[]{:S(2)}) copy-start(f32[48,384]{1,0:T(8,128)} %param.8) | copy-start | bytes 221188
  564.6 22.6 %copy-start.12 = (f32[48,384]{1,0:T(8,128)S(1)}, f32[48,384]{1,0:T(8,128)}, u32[]{:S(2)}) copy-start(f32[48,384]{1,0:T(8,128)} %param.9) | copy-start | bytes 221188
  564.6 224.3 %reduce-scatter.5.cloned.1.call-start = ((), (), s32[]{:S(2)}) async-start(), calls=%async_computation.6 | async-start | bytes 663552 | tf_op jit(solution)/shard_map/reduce_scatter | solution.py:73
  564.9 1.0 copy-start.2
  587.3 27.3 %copy-start.1 = (bf16[3072,384]{1,0:T(8,128)(2,1)S(1)}, bf16[3072,384]{1,0:T(8,128)(2,1)}, u32[]{:S(2)}) copy-start(bf16[3072,384]{1,0:T(8,128)(2,1)} %all-gather.11.cloned.1.call-done) | copy-start | bytes 7077892
  617.3 260.7 %all-reduce.8.cloned.1.call-start = ((), (), s32[]{:S(2)}) async-start(), calls=%async_computation.10 | async-start | bytes 2359296 | tf_op jit(solution)/shard_map/psum | solution.py:95
  679.4 246.3 %copy-start.3 = (bf16[192,3072]{1,0:T(8,128)(2,1)S(1)}, bf16[192,3072]{1,0:T(8,128)(2,1)}, u32[]{:S(2)}) copy-start(bf16[192,3072]{1,0:T(8,128)(2,1)} %all-gather.21.cloned.1.call-done) | copy-start | bytes 3538948
  682.5 243.1 %all-gather.23.cloned.1.call-start = ((), (), s32[]{:S(2)}) async-start(), calls=%async_computation.18 | async-start | bytes 2506752 | tf_op jit(solution)/shard_map/all_gather | solution.py:117
Sparse Core Ops, SparseCore 0:
  24.2 77.5 reduce-scatter.6
  104.0 24.8 all-gather.12
  131.6 54.4 all-gather.14
  260.0 20.8 all-gather.16
  284.7 75.7 reduce-scatter.8
  363.1 45.5 all-gather.18
  411.6 54.1 all-reduce.3
  468.0 45.9 all-gather.8
  516.2 22.8 all-gather.20
  541.6 45.6 all-gather.10
  590.6 86.8 all-reduce.5
  680.6 75.1 reduce-scatter.10
  758.2 30.7 reduce-scatter.4
  792.1 85.8 all-reduce.7
  880.6 45.0 all-gather.22
where the time goes:
time: 936 us; the launch traced here: 935 us
  waiting for transfers between devices  684 us (73%)
  blocking collectives  179 us (19%)
  matrix products  46.3 us (5%)
  between operations  15.6 us (2%)
    reduce_scatter x2, waiting for transfers between devices, local(): lax.psum_scatter(jnp.dot(iterate_rows.T, rounded_iterate, preferred_eleme...  149 us
    psum x2, waiting for transfers between devices, local(): lax.psum(partial_gram.astype(jnp.bfloat16), 'shard').astype(jnp.float32)  148 us
    reduce_scatter x1, waiting for transfers between devices, local(): lax.psum_scatter(jnp.dot(grad_rows.T, gradient, preferred_element_type=jn...  77.6 us
    all_gather x2, waiting for transfers between devices, local(): lax.all_gather(mixing, 'shard', axis=0, tiled=True)  66 us
    psum x1, blocking collectives, local(): total_right = lax.psum(local_right, ('shard', 'tensor'))  64.5 us
    all_gather x1, waiting for transfers between devices, local(): lax.all_gather(right_q, 'shard', axis=0, tiled=True)  57.2 us
    psum x1, waiting for transfers between devices, local(): lax.psum(left_terms.astype(jnp.bfloat16), 'tensor').astype(jnp.float32)  53.3 us
    all_gather x1, waiting for transfers between devices, local(): basis_all = lax.all_gather(basis_left, 'shard', axis=0, tiled=True)  47.2 us
  transfers between devices with their start and end apart: 15, of which 14 were waited for; matrix products, arithmetic and copies ran while one was open for 4% of the time, Pallas kernels for 0%

commit v1 on v0

v1 whole, which is shorter than its diff:
```python
import functools
import math

import jax
import jax.numpy as jnp
from jax import lax
from jax.experimental import pallas as pl
from jax.experimental.pallas import tpu as pltpu
from jax.sharding import PartitionSpec as P

D = 768
FF = 3072
BF = jnp.bfloat16
F32 = jnp.float32
MESH = pl.DeviceIdType.MESH

beta = 0.95
correction = 1.0 - 0.95**10
adam_eps = 1e-08


class Move:
    def __init__(self, copy, landing):
        self.copy, self.landing = copy, landing

    def recv(self):
        self.landing.wait_recv()


class Net:
    def __init__(self, send_sem, recv_sem):
        self.send_sem, self.recv_sem = send_sem, recv_sem
        self.count = 0
        self.sent = []
        s, t = lax.axis_index("shard"), lax.axis_index("tensor")
        self.s, self.t = s, t
        self.z, self.x = s // 4, s % 4
        self.y, self.c = t // 2, t % 2

    def nbr(self, d):
        s, t = self.s, self.t
        z, x, y, c = self.z, self.x, self.y, self.c
        if d == "c":
            return (s, y * 2 + 1 - c)
        step = 1 if d[0] == "+" else 3
        if d[1] == "x":
            return (z * 4 + (x + step) % 4, t)
        if d[1] == "z":
            return (((z + step) % 4) * 4 + x, t)
        return (s, ((y + step) % 4) * 2 + c)

    def barrier(self, dirs):
        sem = pltpu.get_barrier_semaphore()
        for d in dirs:
            pl.semaphore_signal(sem, inc=1, device_id=self.nbr(d), device_id_type=MESH)
        pl.semaphore_wait(sem, len(dirs))

    def send(self, src, dst, landing, d):
        k = self.count
        self.count += 1
        mk = lambda a, b: pltpu.make_async_remote_copy(
            src_ref=a,
            dst_ref=b,
            send_sem=self.send_sem.at[k],
            recv_sem=self.recv_sem.at[k],
            device_id=self.nbr(d),
            device_id_type=MESH,
        )
        copy = mk(src, dst)
        copy.start()
        self.sent.append(copy)
        return Move(copy, mk(landing, landing))

    def drain(self):
        for copy in self.sent:
            copy.wait_send()
        self.sent = []


def cuts(rows):
    if rows % 64 == 0:
        q = rows // 4
        return ((0, q, 2 * q), (2 * q, 3 * q, 4 * q))
    if rows == 48:
        return ((0, 16, 32), (32, 48, 48))
    return ((0, rows, rows), None)


class ShardGather:
    def __init__(self, net, src, buf):
        self.net, self.src, self.buf = net, src, buf
        self.flows = [(i, f) for i, f in enumerate(cuts(src.shape[0])) if f is not None]
        self.m = {}

    def view(self, blk, lo, hi):
        n = self.net
        return self.buf.at[(n.z + blk[0]) % 4, (n.x + blk[1]) % 4, pl.ds(lo, hi - lo), :]

    def axes(self, i):
        return ("x", "z") if i == 0 else ("z", "x")

    def rel(self, i, first, second):
        return (second, first) if i == 0 else (first, second)

    def go(self, i, stage, sgn, first, second, lo, hi, key, own=False):
        if hi == lo:
            return
        axis = self.axes(i)[stage]
        d = ("+" if sgn > 0 else "-") + axis
        blk = self.rel(i, first, second)
        lf, ls = (first - sgn, second) if stage == 0 else (first, second - sgn)
        src = self.src.at[pl.ds(lo, hi - lo), :] if own else self.view(blk, lo, hi)
        self.m[key] = self.net.send(src, self.view(blk, lo, hi), self.view(self.rel(i, lf, ls), lo, hi), d)

    def wait(self, *key):
        if key in self.m:
            self.m[key].recv()

    def start(self):
        n = self.net
        for i, (lo, mid, hi) in self.flows:
            for sgn in (1, -1):
                self.go(i, 0, sgn, 0, 0, lo, hi, (i, "a", sgn), own=True)
        for i, (lo, mid, hi) in self.flows:
            for sgn in (1, -1):
                self.go(i, 1, sgn, 0, 0, lo, hi, (i, "b", 0, sgn), own=True)

    def local(self, sem):
        n = self.net
        self.mine = pltpu.make_async_copy(self.src, self.buf.at[n.z, n.x], sem)
        self.mine.start()

    def second(self, i, first, lo, hi):
        for sgn in (1, -1):
            self.go(i, 1, sgn, first, 0, lo, hi, (i, "b", first, sgn))

    def relay(self, i, first, lo, mid, hi):
        for sgn in (1, -1):
            self.wait(i, "b", first, sgn)
            a, b = (lo, mid) if sgn > 0 else (mid, hi)
            self.go(i, 1, sgn, first, -sgn, a, b, (i, "bb", first, sgn))

    def step1(self):
        for i, (lo, mid, hi) in self.flows:
            for sgn in (1, -1):
                self.wait(i, "a", sgn)
                a, b = (lo, mid) if sgn > 0 else (mid, hi)
                self.go(i, 0, sgn, -sgn, 0, a, b, (i, "aa", sgn))
                self.second(i, -sgn, lo, hi)

    def step2(self):
        for i, (lo, mid, hi) in self.flows:
            self.relay(i, 0, lo, mid, hi)
        for i, (lo, mid, hi) in self.flows:
            self.wait(i, "aa", 1)
            self.wait(i, "aa", -1)
            self.second(i, 2, lo, hi)

    def step3(self):
        for i, (lo, mid, hi) in self.flows:
            for first in (1, -1, 2):
                self.relay(i, first, lo, mid, hi)

    def finish(self):
        for i, _ in self.flows:
            for first in (0, 1, -1, 2):
                for sgn in (1, -1):
                    self.wait(i, "bb", first, sgn)
        self.mine.wait()


class TensorGather:
    def __init__(self, net, src, buf):
        self.net, self.src, self.buf = net, src, buf
        rows = src.shape[0]
        self.cut = (0, rows // 32 * 16, rows)

    def view(self, dy, other, lo, hi):
        n = self.net
        return self.buf.at[(n.y + dy) % 4, (1 - n.c) if other else n.c, pl.ds(lo, hi - lo), :]

    def start(self):
        n = self.net
        hi = self.cut[2]
        self.a = {
            sgn: n.send(self.src, self.view(0, 0, 0, hi), self.view(-sgn, 0, 0, hi), "+y" if sgn > 0 else "-y")
            for sgn in (1, -1)
        }
        self.sib = [n.send(self.src, self.view(0, 0, 0, hi), self.view(0, 1, 0, hi), "c")]

    def local(self, sem):
        n = self.net
        self.mine = pltpu.make_async_copy(self.src, self.buf.at[n.y, n.c], sem)
        self.mine.start()

    def pair(self, dy):
        n, hi = self.net, self.cut[2]
        self.sib.append(n.send(self.view(dy, 0, 0, hi), self.view(dy, 0, 0, hi), self.view(dy, 1, 0, hi), "c"))

    def step1(self):
        n = self.net
        lo, mid, hi = self.cut
        self.aa = []
        for sgn in (1, -1):
            self.a[sgn].recv()
            a, b = (lo, mid) if sgn > 0 else (mid, hi)
            self.aa.append(
                n.send(self.view(-sgn, 0, a, b), self.view(-sgn, 0, a, b), self.view(2, 0, a, b), "+y" if sgn > 0 else "-y")
            )
            self.pair(-sgn)

    def step2(self):
        for m in self.aa:
            m.recv()
        self.pair(2)

    def finish(self):
        for m in self.sib:
            m.recv()
        self.mine.wait()


def run_kernel(body, name, ident, outs, args, scratch, sems):
    def kernel(*refs):
        nin, nout = len(args), len(outs)
        body(refs[:nin], refs[nin : nin + nout], refs[nin + nout :])

    kernel.__name__ = name
    vm = pl.BlockSpec(memory_space=pltpu.VMEM)
    return pl.pallas_call(
        kernel,
        out_shape=[jax.ShapeDtypeStruct(shape, dtype) for shape, dtype in outs],
        in_specs=[vm] * len(args),
        out_specs=[vm] * len(outs),
        scratch_shapes=list(scratch)
        + [
            pltpu.SemaphoreType.DMA((sems,)),
            pltpu.SemaphoreType.DMA((sems,)),
            pltpu.SemaphoreType.DMA((8,)),
        ],
        compiler_params=pltpu.CompilerParams(
            collective_id=ident, has_side_effects=True, vmem_limit_bytes=48 * 2**20
        ),
        name=name,
    )(*args)


PLANE = ("+x", "-x", "+z", "-z")
LINE = ("+y", "-y", "c")


def run_gathers(gathers, lsem):
    for g in gathers:
        g.start()
    for k, g in enumerate(gathers):
        g.local(lsem.at[k])
    for g in gathers:
        g.step1()
    for g in gathers:
        g.step2()
    for g in gathers:
        if isinstance(g, ShardGather):
            g.step3()
    for g in gathers:
        g.finish()


def gather_kernel(name, ident, shard_args, tensor_args):
    args = list(shard_args) + list(tensor_args)
    ns = len(shard_args)
    outs = [((4, 4) + a.shape, a.dtype) for a in shard_args] + [((4, 2) + a.shape, a.dtype) for a in tensor_args]
    dirs = (PLANE if shard_args else ()) + (LINE if tensor_args else ())

    def body(ins, out, rest):
        net = Net(rest[-3], rest[-2])
        net.barrier(dirs)
        gs = [TensorGather(net, ins[k], out[k]) for k in range(ns, len(args))]
        gs += [ShardGather(net, ins[k], out[k]) for k in range(ns)]
        run_gathers(gs, rest[-1])
        net.drain()

    return run_kernel(body, name, ident, outs, args, [], 40 * ns + 8 * len(tensor_args))


def broadcast_line(net, src, dst, lsem):
    rows = src.shape[0]
    half = rows // 2
    k = net.count
    net.count += 5
    dy = (net.y - net.z + 4) % 4
    main = net.c == net.x // 2

    def mk(j, a, lo, hi, d):
        return pltpu.make_async_remote_copy(
            src_ref=a.at[pl.ds(lo, hi - lo), :],
            dst_ref=dst.at[pl.ds(lo, hi - lo), :],
            send_sem=net.send_sem.at[k + j],
            recv_sem=net.recv_sem.at[k + j],
            device_id=net.nbr(d),
            device_id_type=MESH,
        )

    @pl.when(main)
    def _():
        @pl.when(dy == 0)
        def _():
            plus, minus, sib = mk(0, src, 0, rows, "+y"), mk(1, src, 0, rows, "-y"), mk(4, src, 0, rows, "c")
            plus.start()
            minus.start()
            sib.start()
            mine = pltpu.make_async_copy(src, dst, lsem)
            mine.start()
            mine.wait()
            plus.wait_send()
            minus.wait_send()
            sib.wait_send()

        @pl.when(dy == 1)
        def _():
            mk(0, dst, 0, rows, "+y").wait_recv()
            on, sib = mk(2, dst, 0, half, "+y"), mk(4, dst, 0, rows, "c")
            on.start()
            sib.start()
            on.wait_send()
            sib.wait_send()

        @pl.when(dy == 3)
        def _():
            mk(1, dst, 0, rows, "-y").wait_recv()
            on, sib = mk(3, dst, half, rows, "-y"), mk(4, dst, 0, rows, "c")
            on.start()
            sib.start()
            on.wait_send()
            sib.wait_send()

        @pl.when(dy == 2)
        def _():
            mk(2, dst, 0, half, "+y").wait_recv()
            mk(3, dst, half, rows, "-y").wait_recv()
            sib = mk(4, dst, 0, rows, "c")
            sib.start()
            sib.wait_send()

    @pl.when(jnp.logical_not(main))
    def _():
        mk(4, dst, 0, rows, "c").wait_recv()


def line_kernel(name, ident, own, tensor_args):
    args = [own] + list(tensor_args)
    outs = [(own.shape, own.dtype)] + [((4, 2) + a.shape, a.dtype) for a in tensor_args]

    def body(ins, out, rest):
        net = Net(rest[-3], rest[-2])
        net.barrier(LINE)
        gs = [TensorGather(net, ins[k], out[k]) for k in range(1, len(args))]
        for g in gs:
            g.start()
        for j, g in enumerate(gs):
            g.local(rest[-1].at[j + 1])
        for g in gs:
            g.step1()
        broadcast_line(net, ins[0], out[0], rest[-1].at[0])
        for g in gs:
            g.step2()
        for g in gs:
            g.finish()
        net.drain()

    return run_kernel(body, name, ident, outs, args, [], 5 + 8 * len(tensor_args))


def add_into(a, b):
    a[...] = (a[...].astype(F32) + b[...].astype(F32)).astype(a.dtype)


class RingScatter:
    def __init__(self, net, axis, pick, half, first, second):
        self.net, self.axis, self.pick, self.half = net, axis, pick, half
        self.first, self.second = first, second

    def start(self):
        n = self.net
        self.one = [
            n.send(self.half(self.pick(2), h), self.first[h], self.first[h], ("+", "-")[h] + self.axis) for h in (0, 1)
        ]

    def middle(self):
        n = self.net
        self.two = []
        for h, rel in ((0, 1), (1, -1)):
            self.one[h].recv()
            add_into(self.half(self.pick(rel), h), self.first[h])
            self.two.append(n.send(self.pick(rel), self.second[h], self.second[h], ("+", "-")[h] + self.axis))

    def total(self):
        for m in self.two:
            m.recv()
        own = self.pick(0)
        return own[...].astype(F32) + self.second[0][...].astype(F32) + self.second[1][...].astype(F32)


def plane_scatter(net, part, out, rest):
    z, x = net.z, net.x
    rows, cols = part.shape[2], part.shape[3]
    h = rows // 2
    f1, f2, q, g1, g2 = rest[:5]
    zx = (z, x)
    stages = []
    for i in (0, 1):
        lo = i * h

        def pick(rel, i=i, lo=lo):
            if i == 0:
                return part.at[(z + rel) % 4, :, pl.ds(lo, h), :]
            return part.at[:, (x + rel) % 4, pl.ds(lo, h), :]

        def half(view, k):
            return view.at[pl.ds(2 * k, 2)]

        stages.append(
            RingScatter(net, "zx"[i], pick, half, [f1.at[i, 0], f1.at[i, 1]], [f2.at[i, 0], f2.at[i, 1]])
        )
    for r in stages:
        r.start()
    for r in stages:
        r.middle()
    later = []
    for i, r in enumerate(stages):
        q[i] = r.total().astype(q.dtype)

        def pick(rel, i=i):
            return q.at[i, (zx[1 - i] + rel) % 4]

        def half(view, k):
            return view.at[pl.ds(k * (h // 2), h // 2), :]

        later.append(
            RingScatter(net, "xz"[i], pick, half, [g1.at[i, 0], g1.at[i, 1]], [g2.at[i, 0], g2.at[i, 1]])
        )
        later[-1].start()
    for r in later:
        r.middle()
    for i, r in enumerate(later):
        out[pl.ds(i * h, h), :] = r.total()


def scatter_kernel(name, ident, part, tiles):
    rows, cols = part.shape[2:]
    h = rows // 2
    args = [part] + list(tiles)
    outs = [((rows, cols), F32)] + [((4, 4) + a.shape, a.dtype) for a in tiles]
    scratch = [
        pltpu.VMEM((2, 2, 2, h, cols), BF),
        pltpu.VMEM((2, 2, 4, h, cols), BF),
        pltpu.VMEM((2, 4, h, cols), BF),
        pltpu.VMEM((2, 2, h // 2, cols), BF),
        pltpu.VMEM((2, 2, h, cols), BF),
    ]

    def body(ins, out, rest):
        net = Net(rest[-3], rest[-2])
        net.barrier(PLANE)
        gs = [ShardGather(net, ins[k], out[k]) for k in range(1, len(args))]
        for g in gs:
            g.start()
        for j, g in enumerate(gs):
            g.local(rest[-1].at[j])
        plane_scatter(net, ins[0], out[0], rest)
        for g in gs:
            g.step1()
        for g in gs:
            g.step2()
        for g in gs:
            g.step3()
        for g in gs:
            g.finish()
        net.drain()

    return run_kernel(body, name, ident, outs, args, scratch, 16 + 20 * len(tiles))


def line_scatter(net, part, out, rest):
    y, c = net.y, net.c
    g0, q, g1, g2 = rest[:4]
    rows = part.shape[2]
    m = net.send(part.at[1 - c], g0, g0, "c")
    m.recv()
    q[...] = (part[c].astype(F32) + g0[...].astype(F32)).astype(q.dtype)
    cut = rows // 32 * 16

    def pick(rel):
        return q.at[(y + rel) % 4]

    def half(view, k):
        return view.at[pl.ds(0, cut), :] if k == 0 else view.at[pl.ds(cut, rows - cut), :]

    ring = RingScatter(net, "y", pick, half, [g1.at[pl.ds(0, cut)], g1.at[pl.ds(cut, rows - cut)]], [g2.at[0], g2.at[1]])
    ring.start()
    yield
    ring.middle()
    yield
    out[...] = ring.total().astype(out.dtype)


def power_kernel(name, ident, part, block):
    rows, cols = part.shape[2:]
    outs = [((rows, cols), BF), ((4, 2) + block.shape, block.dtype)]
    scratch = [
        pltpu.VMEM((4, rows, cols), BF),
        pltpu.VMEM((4, rows, cols), BF),
        pltpu.VMEM((rows, cols), BF),
        pltpu.VMEM((2, rows, cols), BF),
    ]

    def body(ins, out, rest):
        net = Net(rest[-3], rest[-2])
        net.barrier(LINE)
        g = TensorGather(net, ins[1], out[1])
        g.start()
        g.local(rest[-1].at[0])
        steps = line_scatter(net, ins[0], out[0], rest)
        next(steps)
        g.step1()
        next(steps)
        g.step2()
        for _ in steps:
            pass
        g.finish()
        net.drain()

    return run_kernel(body, name, ident, outs, [part, block], scratch, 16)


def dot(a, b):
    return jnp.dot(a, b, preferred_element_type=F32)


def rows_dot(blocks, cols):
    wide = blocks.reshape(8, blocks.shape[2], blocks.shape[3]).transpose(1, 0, 2).reshape(blocks.shape[2], -1)
    return dot(wide, cols)


def gram_terms(blocks, own):
    b = blocks.reshape(8, blocks.shape[2], blocks.shape[3])
    out = jnp.einsum("tri,rj->tij", b, own, preferred_element_type=F32)
    return out.astype(BF).reshape(4, 4, FF // 16, own.shape[1])


def local(gradient, moment_one, moment_two, stat_left, stat_right, basis_left, basis_right):
    s = lax.axis_index("shard")
    rows_left = gradient.shape[0]
    left_q = (basis_left / math.sqrt(D)).astype(BF)
    right_q = (basis_right / math.sqrt(FF)).astype(BF)
    grad_cols, left_all, right_cols = gather_kernel("gather_in", 0, [gradient, left_q, right_q], [])
    grad_cols = grad_cols.reshape(D, -1)
    left_all = left_all.reshape(D, D)
    right_cols = right_cols.reshape(FF, -1)
    width = FF // 16
    give = jnp.where(s % 2 == 0, grad_cols[:, :width], grad_cols[:, width:])
    own_cols = lax.dynamic_slice_in_dim(left_all, s * rows_left, rows_left, 1)
    half = dot(own_cols.T, grad_cols).astype(BF)
    left_terms = dot(gradient, grad_cols.T).astype(BF)
    grad_rows, half_rows, left_parts = line_kernel("line_in", 1, give, [half, left_terms])
    new_stat_right = beta * stat_right + (1.0 - beta) * (dot(grad_rows.T, grad_cols) / D)
    gram_rows = jnp.sum(left_parts.reshape(8, rows_left, D).astype(F32), axis=0)
    new_stat_left = beta * stat_left + (1.0 - beta) * (gram_rows / FF)
    rotated = rows_dot(half_rows, right_cols)
    new_moment_one = beta * moment_one + (1.0 - beta) * rotated
    new_moment_two = beta * moment_two + (1.0 - beta) * (rotated * rotated)
    direction = (
        new_moment_one / correction / (jnp.sqrt(new_moment_two / correction) + adam_eps)
    ).astype(BF)
    power_left = dot(new_stat_left.astype(BF), left_all).astype(BF)
    dir_cols, power_left_all, stat_rows = gather_kernel(
        "gather_mid", 2, [direction, power_left], [new_stat_right.astype(BF)]
    )
    back_half = dot(left_q, dir_cols.reshape(D, -1)).astype(BF)
    back_terms = dot(back_half, right_cols.T).astype(BF)
    back_terms = back_terms.reshape(rows_left, 4, 2, -1).transpose(2, 1, 0, 3)
    power = rows_dot(stat_rows, right_cols)
    power_b = power.astype(BF)
    update, power_rows = power_kernel("line_mid", 3, back_terms, power_b)

    terms = gram_terms(power_rows, power_b)
    squares = jnp.sum(jnp.square(power_rows.astype(F32)))
    gram, tiles = scatter_kernel("scatter_one", 4, terms, [jnp.broadcast_to(squares, (8, 128))])
    total = jnp.sum(tiles[:, :, 0, 0])
    scale = math.sqrt(FF) / (4.0 * jnp.sqrt(total))
    gram_b = (gram * (scale * scale)).astype(BF)
    (gram_cols,) = gather_kernel("gather_one", 5, [gram_b], [])
    iterate = scale * (1.5 * power - 0.5 * rows_dot(power_rows, gram_cols.reshape(FF, -1)))
    iterate_b = iterate.astype(BF)
    (iterate_rows,) = gather_kernel("line_two", 6, [], [iterate_b])
    (gram,) = scatter_kernel("scatter_two", 7, gram_terms(iterate_rows, iterate_b), [])
    (gram_cols,) = gather_kernel("gather_two", 8, [gram.astype(BF)], [])
    iterate = 1.5 * iterate - 0.5 * rows_dot(iterate_rows, gram_cols.reshape(FF, -1))

    whole = power_left_all.reshape(D, D).astype(F32)
    whole = whole * (math.sqrt(D) / (4.0 * jnp.sqrt(jnp.sum(whole * whole))))
    wb = whole.astype(BF)
    gl = dot(wb.T, wb).astype(BF)
    whole = 1.5 * whole - 0.5 * dot(wb, gl)
    wb = whole.astype(BF)
    gl = dot(wb.T, wb).astype(BF)
    own = lax.dynamic_slice_in_dim(whole, s * rows_left, rows_left, 0)
    left = 1.5 * own - 0.5 * dot(own.astype(BF), gl)
    return (
        update,
        new_moment_one,
        new_moment_two,
        new_stat_left,
        new_stat_right,
        left * math.sqrt(D),
        iterate * math.sqrt(FF),
    )


def solution(mesh):
    both, row = P("shard", "tensor"), P("shard", None)
    return jax.shard_map(
        local,
        mesh=mesh,
        in_specs=(both, both, both, row, both, row, both),
        out_specs=(both, both, both, row, both, row, both),
        check_vma=False,
    )
```

time: 936 us -> 236 us (0.25)
  waiting for transfers between devices: 684 us -> 0 us
  Pallas kernels: 0 us -> 195 us
  blocking collectives: 179 us -> 0 us
  matrix products: 46.3 us -> 21.9 us
  between operations: 15.6 us -> 2.43 us
    reduce_scatter x4 -> x0, waiting for transfers between devices: 258 us -> none  [the longest x2 149 us: local(): lax.psum_scatter(jnp.dot(iterate_rows.T, rounded_iterate, preferred_eleme...]
    all_gather x8 -> x0, waiting for transfers between devices: 224 us -> none  [the longest x2 66 us: local(): lax.all_gather(mixing, 'shard', axis=0, tiled=True)]
    psum x3 -> x0, waiting for transfers between devices: 201 us -> none  [the longest x2 148 us: local(): lax.psum(partial_gram.astype(jnp.bfloat16), 'shard').astype(jnp.float32)]
    pallas_call x0 -> x9, Pallas kernels: none -> 195 us  [run_kernel(): pl.pallas_call(kernel, out_shape=[jax.ShapeDtypeStruct(shape, dtype) for...]
    psum x2 -> x0, blocking collectives: 104 us -> none  [the longest x1 64.5 us: local(): total_right = lax.psum(local_right, ('shard', 'tensor'))]
    all_gather x4 -> x0, blocking collectives: 75 us -> none  [the longest x1 24.4 us: local(): lax.all_gather(direction, 'shard', axis=0, tiled=True)]
    dot_general x15 -> x13, matrix products: 46.3 us -> 21.9 us  [the longest x11 19.8 us: dot(): return jnp.dot(a, b, preferred_element_type=F32)]
  transfers between devices with their start and end apart: 15 -> 0, of which waited for: 14 -> 0; matrix products, arithmetic and copies ran while one was open for 4% -> 0% of each run, Pallas kernels for 0% -> 0%
where the time goes in v1:
time: 236 us
  Pallas kernels  195 us (83%)
  matrix products  21.9 us (9%)
  local copies, waits for them, and re-layouts  8.71 us (4%)
  other arithmetic  7.09 us (3%)
  between operations  2.43 us (1%)
    pallas_call x9, Pallas kernels, run_kernel(): pl.pallas_call(kernel, out_shape=[jax.ShapeDtypeStruct(shape, dtype) for...  195 us
    dot_general x11, matrix products, dot(): return jnp.dot(a, b, preferred_element_type=F32)  19.8 us
    unnamed x25, local copies, waits for them, and re-layouts  5.17 us

profile of v1, /device:TPU:0, one launch (start us, length us, event | category | flops | bytes accessed | tf_op | source)
XLA Modules:
  0.0 235.5 jit_solution(16357931042751353808)
XLA Ops:
  0.6 0.9 multiply_convert_fusion.2.refs_1_
  1.6 1.0 multiply_convert_fusion.1.refs_2_
  2.6 0.8 copy-done.3
  3.4 32.6 %gather_in.1 = (bf16[4,4,48,384]{3,2,1,0:T(8,128)(2,1)S(1)}, bf16[4,4,48,768]{3,2,1,0:T(8,128)(2,1)S(1)}, bf16[4,4,192,384]{3,2,1,0:T(8,128)(2,1)S(1)}) custom-call(bf16[48,384]{1,0:T(8,128)(2,1)S(1)} %copy-done.3, bf16[48,768]{1,0:T(8,128)(2,1)S(1)} %multiply_convert_fusion.2.refs_1_, bf16[192,384]{1,0:T(8,128)(2,1)S(1)} %multiply_convert_fusion.1.refs_2_), custom_call_target="tpu_custom_call" | custom-call | tf_op jit(solution)/shard_map/gather_in/pallas_call | solution.py:230
  36.9 14.2 %line_in.1 = (bf16[768,192]{1,0:T(8,128)(2,1)S(1)}, bf16[4,2,48,384]{3,2,1,0:T(8,128)(2,1)S(1)}, bf16[4,2,48,768]{3,2,1,0:T(8,128)(2,1)S(1)}) custom-call(bf16[768,192]{1,0:T(8,128)(2,1)S(1)} %slice_select_fusion.refs_0_, bf16[48,384]{1,0:T(8,128)(2,1)S(1)} %convolution_convert_fusion.7.refs_1_, bf16[48,768]{1,0:T(8,128)(2,1)S(1)} %fusion.20.refs_2_), custom_call_target="tpu_custom_call" | custom-call | tf_op jit(solution)/shard_map/line_in/pallas_call | solution.py:230
  51.1 1.1 fusion.27
  52.3 1.2 divide_convert_fusion
  53.9 30.0 %gather_mid.1 = (bf16[4,4,48,384]{3,2,1,0:T(8,128)(2,1)S(1)}, bf16[4,4,48,768]{3,2,1,0:T(8,128)(2,1)S(1)}, bf16[4,2,192,384]{3,2,1,0:T(8,128)(2,1)S(1)}) custom-call(bf16[48,384]{1,0:T(8,128)(2,1)S(1)} %get-tuple-element.33.refs_0_, bf16[48,768]{1,0:T(8,128)(2,1)S(1)} %convolution_convert_fusion.4.refs_1_, bf16[192,384]{1,0:T(8,128)(2,1)S(1)} %get-tuple-element.38.refs_2_), custom_call_target="tpu_custom_call" | custom-call | tf_op jit(solution)/shard_map/gather_mid/pallas_call | solution.py:230
  83.9 1.0 copy-done
  85.0 0.8 copy-done.2
  85.8 1.2 fusion.2
  87.7 2.8 %convolution_convert_fusion = bf16[48,3072]{1,0:T(8,128)(2,1)} fusion(bf16[3072,384]{1,0:T(8,128)(2,1)S(1)} %bitcast.75, bf16[48,768]{1,0:T(8,128)(2,1)} %copy-done.1, bf16[768,384]{1,0:T(8,128)(2,1)} %bitcast.93), kind=kOutput, calls=%fused_computation | convolution fusion | flops 141723648 | bytes 3317760 | tf_op jit(solution)/shard_map/dot_general | solution.py:536
  90.5 1.9 reshape.83
  92.4 1.0 copy.29
  93.4 1.5 copy.21
  94.9 1.5 fusion.28
  96.4 11.0 %line_mid.1 = (bf16[48,384]{1,0:T(8,128)(2,1)S(1)}, bf16[4,2,192,384]{3,2,1,0:T(8,128)(2,1)S(1)}) custom-call(bf16[2,4,48,384]{3,2,1,0:T(8,128)(2,1)S(1)} %bitcast.92, bf16[192,384]{1,0:T(8,128)(2,1)S(1)} %get-tuple-element.40.refs_1_), custom_call_target="tpu_custom_call" | custom-call | tf_op jit(solution)/shard_map/line_mid/pallas_call | solution.py:230
  107.4 1.2 multiply_reduce_fusion
  108.6 0.6 broadcast_in_dim.3.refs_1_
  109.5 1.0 convolution_convert_fusion.2
  110.5 32.9 %scatter_one.1 = (f32[192,384]{1,0:T(8,128)S(1)}, f32[4,4,8,128]{3,2,1,0:T(8,128)S(1)}) custom-call(bf16[4,4,192,384]{3,2,1,0:T(8,128)(2,1)S(1)} %bitcast.86, f32[8,128]{1,0:T(8,128)S(1)} %broadcast_in_dim.3.refs_1_), custom_call_target="tpu_custom_call" | custom-call | tf_op jit(solution)/shard_map/scatter_one/pallas_call | solution.py:230
  143.3 0.6 slice_reduce_fusion
  144.7 19.1 %gather_one.1 = bf16[4,4,192,384]{3,2,1,0:T(8,128)(2,1)S(1)} custom-call(bf16[192,384]{1,0:T(8,128)(2,1)S(1)} %multiply_convert_fusion.refs_0_), custom_call_target="tpu_custom_call" | custom-call | tf_op jit(solution)/shard_map/gather_one/pallas_call | solution.py:230
  163.9 0.8 fusion.29
  164.7 11.1 %line_two.1 = bf16[4,2,192,384]{3,2,1,0:T(8,128)(2,1)S(1)} custom-call(bf16[192,384]{1,0:T(8,128)(2,1)S(1)} %get-tuple-element.42.refs_0_), custom_call_target="tpu_custom_call" | custom-call | tf_op jit(solution)/shard_map/line_two/pallas_call | solution.py:230
  176.0 1.0 convolution_convert_fusion.1
  177.1 24.8 %scatter_two.1 = f32[192,384]{1,0:T(8,128)S(1)} custom-call(bf16[4,4,192,384]{3,2,1,0:T(8,128)(2,1)S(1)} %bitcast.87), custom_call_target="tpu_custom_call" | custom-call | tf_op jit(solution)/shard_map/scatter_two/pallas_call | solution.py:230
  201.9 19.7 %gather_two.1 = bf16[4,4,192,384]{3,2,1,0:T(8,128)(2,1)S(1)} custom-call(bf16[192,384]{1,0:T(8,128)(2,1)S(1)} %convert_element_type.109.refs_0_), custom_call_target="tpu_custom_call" | custom-call | tf_op jit(solution)/shard_map/gather_two/pallas_call | solution.py:230
  221.6 1.5 fusion.10
  223.1 1.8 fusion
  224.9 5.5 %bitcast_subtract_fusion = f32[768,768]{1,0:T(8,128)} fusion(f32[4,4,48,768]{3,2,1,0:T(8,128)} %get-tuple-element.37, bf16[768,768]{1,0:T(8,128)(2,1)S(1)} %bitcast.98, bf16[4,4,48,768]{3,2,1,0:T(8,128)(2,1)S(1)} %get-tuple-element.36), kind=kOutput, calls=%fused_computation.7 | convolution fusion | flops 1813708800 | bytes 7077888 | tf_op jit(solution)/shard_map/dot_general | solution.py:536
  230.4 4.5 %fusion.17 = f32[48,768]{1,0:T(8,128)} fusion(f32[768,768]{1,0:T(8,128)} %bitcast_subtract_fusion, s32[]{:T(128)S(6)} %select_n.22), kind=kOutput, calls=%fused_computation.25 | convolution fusion | flops 963956736 | bytes 2802688 | tf_op jit(solution)/shard_map/dot_general | solution.py:536
  (29 shorter events, 2.4 us)
Async XLA Ops:
  1.6 34.8 %copy-start.1 = (bf16[48,768]{1,0:T(8,128)(2,1)}, bf16[48,768]{1,0:T(8,128)(2,1)S(1)}, u32[]{:S(2)}) copy-start(bf16[48,768]{1,0:T(8,128)(2,1)S(1)} %multiply_convert_fusion.2.refs_1_) | copy-start | bytes 221188
  2.6 0.8 copy-start.3
  36.4 14.8 %copy-start.6 = (f32[192,384]{1,0:T(8,128)S(1)}, f32[192,384]{1,0:T(8,128)}, u32[]{:S(2)}) copy-start(f32[192,384]{1,0:T(8,128)} %param.11) | copy-start | bytes 884740
  51.1 1.1 copy-start.8
  51.1 1.1 copy-start.9
  52.3 1.2 copy-start.7
  53.5 30.4 %copy-start.5 = (f32[48,768]{1,0:T(8,128)}, f32[48,768]{1,0:T(8,128)S(1)}, u32[]{:S(2)}) copy-start(f32[48,768]{1,0:T(8,128)S(1)} %multiply_add_fusion) | copy-start | bytes 442372
  83.9 1.0 copy-start
  85.0 0.8 copy-start.2
  144.7 19.2 %copy-start.4 = (f32[192,384]{1,0:T(8,128)S(1)}, f32[192,384]{1,0:T(8,128)}, u32[]{:S(2)}) copy-start(f32[192,384]{1,0:T(8,128)} %get-tuple-element.41) | copy-start | bytes 884740

commit v2 on v1

v2 whole, which is shorter than its diff:
```python
import functools
import math

import jax
import jax.numpy as jnp
from jax import lax
from jax.experimental import pallas as pl
from jax.experimental.pallas import tpu as pltpu
from jax.sharding import PartitionSpec as P

D = 768
FF = 3072
BF = jnp.bfloat16
F32 = jnp.float32
MESH = pl.DeviceIdType.MESH

beta = 0.95
correction = 1.0 - 0.95**10
adam_eps = 1e-08


class Move:
    def __init__(self, copy, landing):
        self.copy, self.landing = copy, landing

    def recv(self):
        self.landing.wait_recv()


class Net:
    def __init__(self, send_sem, recv_sem):
        self.send_sem, self.recv_sem = send_sem, recv_sem
        self.count = 0
        self.sent = []
        s, t = lax.axis_index("shard"), lax.axis_index("tensor")
        self.s, self.t = s, t
        self.z, self.x = s // 4, s % 4
        self.y, self.c = t // 2, t % 2

    def nbr(self, d):
        s, t = self.s, self.t
        z, x, y, c = self.z, self.x, self.y, self.c
        if d == "c":
            return (s, y * 2 + 1 - c)
        step = 1 if d[0] == "+" else 3
        if d[1] == "x":
            return (z * 4 + (x + step) % 4, t)
        if d[1] == "z":
            return (((z + step) % 4) * 4 + x, t)
        return (s, ((y + step) % 4) * 2 + c)

    def barrier(self, dirs):
        sem = pltpu.get_barrier_semaphore()
        for d in dirs:
            pl.semaphore_signal(sem, inc=1, device_id=self.nbr(d), device_id_type=MESH)
        pl.semaphore_wait(sem, len(dirs))

    def send(self, src, dst, landing, d):
        k = self.count
        self.count += 1
        mk = lambda a, b: pltpu.make_async_remote_copy(
            src_ref=a,
            dst_ref=b,
            send_sem=self.send_sem.at[k],
            recv_sem=self.recv_sem.at[k],
            device_id=self.nbr(d),
            device_id_type=MESH,
        )
        copy = mk(src, dst)
        copy.start()
        self.sent.append(copy)
        return Move(copy, mk(landing, landing))

    def drain(self):
        for copy in self.sent:
            copy.wait_send()
        self.sent = []


def cuts(rows):
    if rows % 64 == 0:
        q = rows // 4
        return ((0, q, 2 * q), (2 * q, 3 * q, 4 * q))
    if rows == 48:
        return ((0, 16, 32), (32, 48, 48))
    return ((0, rows, rows), None)


class ShardGather:
    def __init__(self, net, src, buf):
        self.net, self.src, self.buf = net, src, buf
        self.flows = [(i, f) for i, f in enumerate(cuts(src.shape[0])) if f is not None]
        self.m = {}

    def view(self, blk, lo, hi):
        n, rows = self.net, self.src.shape[0]
        slot = (n.z + blk[0]) % 4 * 4 + (n.x + blk[1]) % 4
        return self.buf.at[pl.ds(pl.multiple_of(slot * rows + lo, 8), hi - lo), :]

    def axes(self, i):
        return ("x", "z") if i == 0 else ("z", "x")

    def rel(self, i, first, second):
        return (second, first) if i == 0 else (first, second)

    def go(self, i, stage, sgn, first, second, lo, hi, key, own=False):
        if hi == lo:
            return
        axis = self.axes(i)[stage]
        d = ("+" if sgn > 0 else "-") + axis
        blk = self.rel(i, first, second)
        lf, ls = (first - sgn, second) if stage == 0 else (first, second - sgn)
        src = self.src.at[pl.ds(lo, hi - lo), :] if own else self.view(blk, lo, hi)
        self.m[key] = self.net.send(src, self.view(blk, lo, hi), self.view(self.rel(i, lf, ls), lo, hi), d)

    def wait(self, *key):
        if key in self.m:
            self.m[key].recv()

    def start(self):
        n = self.net
        for i, (lo, mid, hi) in self.flows:
            for sgn in (1, -1):
                self.go(i, 0, sgn, 0, 0, lo, hi, (i, "a", sgn), own=True)
        for i, (lo, mid, hi) in self.flows:
            for sgn in (1, -1):
                self.go(i, 1, sgn, 0, 0, lo, hi, (i, "b", 0, sgn), own=True)

    def local(self, sem):
        n = self.net
        self.mine = pltpu.make_async_copy(self.src, self.view((0, 0), 0, self.src.shape[0]), sem)
        self.mine.start()

    def second(self, i, first, lo, hi):
        for sgn in (1, -1):
            self.go(i, 1, sgn, first, 0, lo, hi, (i, "b", first, sgn))

    def relay(self, i, first, lo, mid, hi):
        for sgn in (1, -1):
            self.wait(i, "b", first, sgn)
            a, b = (lo, mid) if sgn > 0 else (mid, hi)
            self.go(i, 1, sgn, first, -sgn, a, b, (i, "bb", first, sgn))

    def step1(self):
        for i, (lo, mid, hi) in self.flows:
            for sgn in (1, -1):
                self.wait(i, "a", sgn)
                a, b = (lo, mid) if sgn > 0 else (mid, hi)
                self.go(i, 0, sgn, -sgn, 0, a, b, (i, "aa", sgn))
                self.second(i, -sgn, lo, hi)

    def step2(self):
        for i, (lo, mid, hi) in self.flows:
            self.relay(i, 0, lo, mid, hi)
        for i, (lo, mid, hi) in self.flows:
            self.wait(i, "aa", 1)
            self.wait(i, "aa", -1)
            self.second(i, 2, lo, hi)

    def step3(self):
        for i, (lo, mid, hi) in self.flows:
            for first in (1, -1, 2):
                self.relay(i, first, lo, mid, hi)

    def finish(self):
        for i, _ in self.flows:
            for first in (0, 1, -1, 2):
                for sgn in (1, -1):
                    self.wait(i, "bb", first, sgn)
        self.mine.wait()


class TensorGather:
    def __init__(self, net, src, buf):
        self.net, self.src, self.buf = net, src, buf
        rows = src.shape[0]
        self.cut = (0, rows // 32 * 16, rows)

    def view(self, dy, other, lo, hi):
        n, rows = self.net, self.src.shape[0]
        slot = (n.y + dy) % 4 * 2 + ((1 - n.c) if other else n.c)
        return self.buf.at[pl.ds(pl.multiple_of(slot * rows + lo, 16), hi - lo), :]

    def start(self):
        n = self.net
        hi = self.cut[2]
        self.a = {
            sgn: n.send(self.src, self.view(0, 0, 0, hi), self.view(-sgn, 0, 0, hi), "+y" if sgn > 0 else "-y")
            for sgn in (1, -1)
        }
        self.sib = [n.send(self.src, self.view(0, 0, 0, hi), self.view(0, 1, 0, hi), "c")]

    def local(self, sem):
        n = self.net
        self.mine = pltpu.make_async_copy(self.src, self.view(0, 0, 0, self.src.shape[0]), sem)
        self.mine.start()

    def pair(self, dy):
        n, hi = self.net, self.cut[2]
        self.sib.append(n.send(self.view(dy, 0, 0, hi), self.view(dy, 0, 0, hi), self.view(dy, 1, 0, hi), "c"))

    def step1(self):
        n = self.net
        lo, mid, hi = self.cut
        self.aa = []
        for sgn in (1, -1):
            self.a[sgn].recv()
            a, b = (lo, mid) if sgn > 0 else (mid, hi)
            self.aa.append(
                n.send(self.view(-sgn, 0, a, b), self.view(-sgn, 0, a, b), self.view(2, 0, a, b), "+y" if sgn > 0 else "-y")
            )
            self.pair(-sgn)

    def step2(self):
        for m in self.aa:
            m.recv()
        self.pair(2)

    def finish(self):
        for m in self.sib:
            m.recv()
        self.mine.wait()


def add_into(a, b):
    a[...] = (a[...].astype(F32) + b[...].astype(F32)).astype(a.dtype)


class RingScatter:
    def __init__(self, net, axis, pick, half, first, second):
        self.net, self.axis, self.pick, self.half = net, axis, pick, half
        self.first, self.second = first, second

    def start(self):
        n = self.net
        self.one = [
            n.send(self.half(self.pick(2), h), self.first[h], self.first[h], ("+", "-")[h] + self.axis) for h in (0, 1)
        ]

    def middle(self):
        n = self.net
        self.two = []
        for h, rel in ((0, 1), (1, -1)):
            self.one[h].recv()
            add_into(self.half(self.pick(rel), h), self.first[h])
            self.two.append(n.send(self.pick(rel), self.second[h], self.second[h], ("+", "-")[h] + self.axis))

    def total(self):
        for m in self.two:
            m.recv()
        own = self.pick(0)
        return own[...].astype(F32) + self.second[0][...].astype(F32) + self.second[1][...].astype(F32)


class LineBroadcast:
    def __init__(self, net, src, dst, lsem):
        self.net, self.src, self.dst, self.lsem = net, src, dst, lsem
        self.k = net.count
        net.count += 5
        self.dy = (net.y - net.z + 4) % 4
        self.main = net.c == net.x // 2
        self.rows = src.shape[0]

    def msg(self, j, a, lo, hi, d):
        n = self.net
        return pltpu.make_async_remote_copy(
            src_ref=a.at[pl.ds(lo, hi - lo), :],
            dst_ref=self.dst.at[pl.ds(lo, hi - lo), :],
            send_sem=n.send_sem.at[self.k + j],
            recv_sem=n.recv_sem.at[self.k + j],
            device_id=n.nbr(d),
            device_id_type=MESH,
        )

    def at(self, dy):
        return pl.when(jnp.logical_and(self.main, self.dy == dy))

    def start(self):
        r = self.rows

        @self.at(0)
        def _():
            self.msg(0, self.src, 0, r, "+y").start()
            self.msg(1, self.src, 0, r, "-y").start()
            self.msg(4, self.src, 0, r, "c").start()
            pltpu.make_async_copy(self.src, self.dst, self.lsem).start()

    def middle(self):
        r, h = self.rows, self.rows // 2

        @self.at(1)
        def _():
            self.msg(0, self.dst, 0, r, "+y").wait_recv()
            self.msg(2, self.dst, 0, h, "+y").start()
            self.msg(4, self.dst, 0, r, "c").start()

        @self.at(3)
        def _():
            self.msg(1, self.dst, 0, r, "-y").wait_recv()
            self.msg(3, self.dst, h, r, "-y").start()
            self.msg(4, self.dst, 0, r, "c").start()

    def finish(self):
        r, h = self.rows, self.rows // 2

        @self.at(2)
        def _():
            self.msg(2, self.dst, 0, h, "+y").wait_recv()
            self.msg(3, self.dst, h, r, "-y").wait_recv()
            self.msg(4, self.dst, 0, r, "c").start()

        @pl.when(jnp.logical_not(self.main))
        def _():
            self.msg(4, self.dst, 0, r, "c").wait_recv()

        @self.at(0)
        def _():
            pltpu.make_async_copy(self.src, self.dst, self.lsem).wait()
            self.msg(0, self.src, 0, r, "+y").wait_send()
            self.msg(1, self.src, 0, r, "-y").wait_send()

        @self.at(1)
        def _():
            self.msg(2, self.dst, 0, h, "+y").wait_send()

        @self.at(3)
        def _():
            self.msg(3, self.dst, h, r, "-y").wait_send()

        @pl.when(self.main)
        def _():
            self.msg(4, self.dst, 0, r, "c").wait_send()


def plane_scatter(net, part, out, f1, f2, q, g1, g2):
    z, x = net.z, net.x
    h = part.shape[2] // 2
    zx = (z, x)
    stages = []
    for i in (0, 1):
        lo = i * h

        def pick(rel, i=i, lo=lo):
            if i == 0:
                return part.at[(z + rel) % 4, :, pl.ds(lo, h), :]
            return part.at[:, (x + rel) % 4, pl.ds(lo, h), :]

        def half(view, k):
            return view.at[pl.ds(2 * k, 2)]

        stages.append(RingScatter(net, "zx"[i], pick, half, [f1.at[i, 0], f1.at[i, 1]], [f2.at[i, 0], f2.at[i, 1]]))
    for r in stages:
        r.start()
    yield
    for r in stages:
        r.middle()
    yield
    later = []
    for i, r in enumerate(stages):
        q[i] = r.total().astype(q.dtype)

        def pick(rel, i=i):
            return q.at[i, (zx[1 - i] + rel) % 4]

        def half(view, k):
            return view.at[pl.ds(k * (h // 2), h // 2), :]

        later.append(RingScatter(net, "xz"[i], pick, half, [g1.at[i, 0], g1.at[i, 1]], [g2.at[i, 0], g2.at[i, 1]]))
        later[-1].start()
    yield
    for r in later:
        r.middle()
    yield
    for i, r in enumerate(later):
        out[pl.ds(i * h, h), :] = r.total()


def line_scatter(net, part, out, g0, q, g1, g2):
    y, c = net.y, net.c
    rows = part.shape[2]
    m = net.send(part.at[1 - c], g0, g0, "c")
    yield
    m.recv()
    q[...] = (part[c].astype(F32) + g0[...].astype(F32)).astype(q.dtype)
    cut = rows // 32 * 16

    def pick(rel):
        return q.at[(y + rel) % 4]

    def half(view, k):
        return view.at[pl.ds(0, cut), :] if k == 0 else view.at[pl.ds(cut, rows - cut), :]

    ring = RingScatter(net, "y", pick, half, [g1.at[pl.ds(0, cut)], g1.at[pl.ds(cut, rows - cut)]], [g2.at[0], g2.at[1]])
    ring.start()
    yield
    ring.middle()
    yield
    out[...] = ring.total().astype(out.dtype)


def dot(a, b):
    return jnp.dot(a, b, preferred_element_type=F32)


def dot_tn(a, b):
    return lax.dot_general(a, b, (((0,), (0,)), ((), ())), preferred_element_type=F32)


def dot_nt(a, b):
    return lax.dot_general(a, b, (((1,), (1,)), ((), ())), preferred_element_type=F32)


def rows_dot(blocks, cols, acc):
    rows, width = acc.shape[0], blocks.shape[1]
    acc[...] = jnp.zeros_like(acc)

    def step(j, carry):
        a = blocks[pl.ds(pl.multiple_of(j * rows, 16), rows), :]
        acc[...] += dot(a, cols[pl.ds(pl.multiple_of(j * width, 16), width), :])
        return carry

    lax.fori_loop(0, 8, step, 0)


SEMS = 430
ROWS, COLS, LROWS = FF // 16, FF // 8, D // 16
BUFFERS = dict(
    lq=((LROWS, D), BF),
    rq=((ROWS, COLS), BF),
    gcols=((D, COLS), BF),
    lall=((D, D), BF),
    qcols=((FF, COLS), BF),
    gs_own=((D, ROWS), BF),
    gs=((D, ROWS), BF),
    lterms=((LROWS, D), BF),
    lparts=((8 * LROWS, D), BF),
    half_all=((D, COLS), BF),
    half_rows=((8 * LROWS, COLS), BF),
    s_b=((ROWS, COLS), BF),
    s_rows=((8 * ROWS, COLS), BF),
    p=((ROWS, COLS), F32),
    p_b=((ROWS, COLS), BF),
    p_rows=((8 * ROWS, COLS), BF),
    rot=((LROWS, COLS), F32),
    dir_b=((LROWS, COLS), BF),
    dir_cols=((D, COLS), BF),
    pl_own=((LROWS, D), F32),
    pl_b=((LROWS, D), BF),
    pl_all=((D, D), BF),
    gl=((D, D), BF),
    wl=((D, D), BF),
    tile=((8, 128), F32),
    tiles=((128, 128), F32),
    part=((4, 4, ROWS, COLS), BF),
    f1=((2, 2, 2, ROWS // 2, COLS), BF),
    f2=((2, 2, 4, ROWS // 2, COLS), BF),
    fq=((2, 4, ROWS // 2, COLS), BF),
    fg1=((2, 2, ROWS // 4, COLS), BF),
    fg2=((2, 2, ROWS // 2, COLS), BF),
    a=((ROWS, COLS), F32),
    a_b=((ROWS, COLS), BF),
    a_cols=((FF, COLS), BF),
    a_rows=((8 * ROWS, COLS), BF),
    t=((ROWS, COLS), F32),
    t_b=((ROWS, COLS), BF),
    t_cols=((FF, COLS), BF),
    t_rows=((8 * ROWS, COLS), BF),
    w=((ROWS, COLS), F32),
    w_b=((ROWS, COLS), BF),
    w_cols=((FF, COLS), BF),
    upart=((2, 4, LROWS, COLS), BF),
    u0=((4, LROWS, COLS), BF),
    uq=((4, LROWS, COLS), BF),
    u1=((LROWS, COLS), BF),
    u2=((2, LROWS, COLS), BF),
)
NBR = ("+x", "-x", "+z", "-z", "+y", "-y", "c")


def kernel(*refs):
    grad, m1, m2, stat_l, stat_r, basis_l, basis_r = refs[:7]
    update, new_m1, new_m2, new_sl, new_sr, new_bl, new_br = refs[7:14]
    b = dict(zip(BUFFERS, refs[14 : 14 + len(BUFFERS)]))
    send_sem, recv_sem, lsem = refs[14 + len(BUFFERS) :]
    net = Net(send_sem, recv_sem)
    x, s = net.x, net.s
    own_left = pl.ds(pl.multiple_of(s * LROWS, 16), LROWS)
    locals_used = [0]

    def begin(*gathers):
        for g in gathers:
            g.start()
            g.local(lsem.at[locals_used[0]])
            locals_used[0] += 1

    def shard(src, dst):
        return ShardGather(net, src if not isinstance(src, str) else b[src], b[dst])

    def tensor(src, dst):
        return TensorGather(net, b[src], b[dst])

    b["lq"][...] = (basis_l[...] * (1.0 / math.sqrt(D))).astype(BF)
    b["rq"][...] = (basis_r[...] * (1.0 / math.sqrt(FF))).astype(BF)
    net.barrier(NBR)

    g_grad, g_left, g_right = shard(grad, "gcols"), shard("lq", "lall"), shard("rq", "qcols")
    begin(g_grad, g_left)
    g_grad.step1()
    g_left.step1()
    g_grad.step2()
    g_left.step2()
    g_grad.step3()
    g_grad.finish()
    begin(g_right)
    cast = LineBroadcast(net, b["gs_own"], b["gs"], lsem.at[locals_used[0]])
    locals_used[0] += 1
    pick = lax.broadcasted_iota(jnp.int32, (COLS, ROWS), 0) == lax.broadcasted_iota(
        jnp.int32, (COLS, ROWS), 1
    ) + ROWS * (x % 2)
    gcols = b["gcols"][...]
    b["gs_own"][...] = dot(gcols, jnp.where(pick, 1.0, 0.0).astype(BF)).astype(BF)
    cast.start()
    b["lterms"][...] = dot_nt(grad[...], gcols).astype(BF)
    t_lterms = tensor("lterms", "lparts")
    begin(t_lterms)
    g_left.step3()
    g_right.step1()
    cast.middle()
    g_left.finish()
    b["half_all"][...] = dot_tn(b["lall"][...], gcols).astype(BF)
    g_right.step2()
    cast.finish()

    new_sr[...] = beta * stat_r[...] + ((1.0 - beta) / D) * dot_tn(b["gs"][...], gcols)
    b["s_b"][...] = new_sr[...].astype(BF)
    t_stat = tensor("s_b", "s_rows")
    begin(t_stat)
    t_half = TensorGather(net, b["half_all"].at[own_left, :], b["half_rows"])
    begin(t_half)
    t_lterms.step1()
    g_right.step3()
    t_stat.step1()
    t_half.step1()
    t_lterms.step2()
    t_stat.step2()
    t_half.step2()
    g_right.finish()
    t_stat.finish()
    rows_dot(b["s_rows"], b["qcols"], b["p"])
    b["p_b"][...] = b["p"][...].astype(BF)
    t_power = tensor("p_b", "p_rows")
    begin(t_power)

    t_lterms.finish()
    t_half.finish()
    rows_dot(b["half_rows"], b["qcols"], b["rot"])
    rot = b["rot"][...]
    first = beta * m1[...] + (1.0 - beta) * rot
    second = beta * m2[...] + (1.0 - beta) * (rot * rot)
    new_m1[...] = first
    new_m2[...] = second
    b["dir_b"][...] = ((first / correction) / (jnp.sqrt(second / correction) + adam_eps)).astype(BF)
    g_dir = shard("dir_b", "dir_cols")
    begin(g_dir)
    gram = b["lparts"][pl.ds(0, LROWS), :].astype(F32)
    for j in range(1, 8):
        gram += b["lparts"][pl.ds(j * LROWS, LROWS), :].astype(F32)
    new_sl[...] = beta * stat_l[...] + ((1.0 - beta) / FF) * gram
    b["pl_own"][...] = dot(new_sl[...].astype(BF), b["lall"][...])
    b["pl_b"][...] = b["pl_own"][...].astype(BF)
    g_pl = shard("pl_b", "pl_all")
    begin(g_pl)
    t_power.step1()
    g_dir.step1()
    g_pl.step1()
    t_power.step2()
    t_power.finish()

    def squares(j, total):
        v = b["p_rows"][pl.ds(pl.multiple_of(j * 16, 16), 16), :].astype(F32)
        return total + v * v

    def term(j, carry):
        v = dot_tn(b["p_rows"][pl.ds(pl.multiple_of(j * ROWS, 16), ROWS), :], b["p_b"][...]).astype(BF)
        b["part"][j // 2, pl.ds(j % 2 * 2, 2), :, :] = v.reshape(2, ROWS, COLS)
        return carry

    lax.fori_loop(0, 8, term, 0)
    scatter = plane_scatter(net, b["part"], b["a"], b["f1"], b["f2"], b["fq"], b["fg1"], b["fg2"])
    next(scatter)
    total = lax.fori_loop(0, ROWS // 2, squares, jnp.zeros((16, COLS), F32))
    b["tile"][...] = jnp.broadcast_to(jnp.sum(total, keepdims=True), (8, 128))
    g_tile = shard("tile", "tiles")
    begin(g_tile)
    g_dir.step2()
    g_pl.step2()
    next(scatter)
    g_tile.step1()
    g_dir.step3()
    g_pl.step3()
    next(scatter)
    g_tile.step2()
    next(scatter)
    g_tile.step3()
    for _ in scatter:
        pass
    g_tile.finish()
    norm = jnp.sum(b["tiles"][...], keepdims=True) / 1024.0
    scale = math.sqrt(FF) / (4.0 * jnp.sqrt(norm))
    b["a"][...] = b["a"][...] * (scale * scale)
    b["a_b"][...] = b["a"][...].astype(BF)
    g_a, t_a = shard("a_b", "a_cols"), tensor("a_b", "a_rows")
    begin(g_a, t_a)

    g_dir.finish()
    back = dot(b["lq"][...], b["dir_cols"][...]).astype(BF)

    def back_term(j, carry):
        v = dot_nt(back, b["qcols"][pl.ds(pl.multiple_of(j * COLS, 16), COLS), :])
        b["upart"][j % 2, j // 2] = v.astype(BF)
        return carry

    lax.fori_loop(0, 8, back_term, 0)
    to_update = line_scatter(net, b["upart"], update, b["u0"], b["uq"], b["u1"], b["u2"])
    g_a.step1()
    t_a.step1()
    next(to_update)
    g_a.step2()
    t_a.step2()
    next(to_update)

    g_pl.finish()

    def left_squares(j, total):
        v = b["pl_all"][pl.ds(pl.multiple_of(j * 16, 16), 16), :].astype(F32)
        return total + v * v

    left_total = lax.fori_loop(0, D // 16, left_squares, jnp.zeros((16, D), F32))
    left_scale = math.sqrt(D) / (4.0 * jnp.sqrt(jnp.sum(left_total, keepdims=True)))

    def left_gram(ref, factor):
        def step(j, carry):
            cut = pl.ds(pl.multiple_of(j * 128, 128), 128)
            b["gl"][cut, :] = (dot_tn(ref[:, cut], ref[...]) * factor).astype(BF)
            return carry

        lax.fori_loop(0, D // 128, step, 0)

    g_a.step3()
    left_gram(b["pl_all"], left_scale * left_scale)
    next(to_update)
    g_a.finish()
    t_a.finish()
    for _ in to_update:
        pass

    rows_dot(b["a_rows"], b["a_cols"], b["t"])
    b["t_b"][...] = b["t"][...].astype(BF)
    g_t, t_t = shard("t_b", "t_cols"), tensor("t_b", "t_rows")
    begin(g_t, t_t)

    def left_step(j, carry):
        cut = pl.ds(pl.multiple_of(j * 128, 128), 128)
        v = b["pl_all"][cut, :]
        b["wl"][cut, :] = (left_scale * (1.5 * v.astype(F32) - 0.5 * dot(v, b["gl"][...]))).astype(BF)
        return carry

    lax.fori_loop(0, D // 128, left_step, 0)
    b["pl_own"][...] = left_scale * (1.5 * b["pl_own"][...] - 0.5 * dot(b["pl_b"][...], b["gl"][...]))
    g_t.step1()
    t_t.step1()
    g_t.step2()
    t_t.step2()
    g_t.step3()
    t_t.finish()

    def blend(j, carry):
        cut = pl.ds(pl.multiple_of(j * ROWS, 16), ROWS)
        v = -0.5625 * b["a_rows"][cut, :].astype(F32) + 0.0625 * b["t_rows"][cut, :].astype(F32)
        b["t_rows"][cut, :] = v.astype(BF)
        return carry

    net.drain()
    lax.fori_loop(0, 8, blend, 0)
    g_t.finish()

    rows_dot(b["t_rows"], b["t_cols"], b["w"])
    b["w_b"][...] = (b["w"][...] - 2.4375 * b["a"][...] + 1.6875 * b["t"][...]).astype(BF)
    g_w = shard("w_b", "w_cols")
    begin(g_w)
    left_gram(b["wl"], 1.0)
    mine = b["pl_own"][...]
    new_bl[...] = math.sqrt(D) * (1.5 * mine - 0.5 * dot(mine.astype(BF), b["gl"][...]))
    g_w.step1()
    g_w.step2()
    g_w.step3()
    g_w.finish()
    rows_dot(b["p_rows"], b["w_cols"], b["w"])
    new_br[...] = (math.sqrt(FF) * scale) * (2.25 * b["p"][...] + b["w"][...])
    net.drain()


def local(gradient, moment_one, moment_two, stat_left, stat_right, basis_left, basis_right):
    args = (gradient, moment_one, moment_two, stat_left, stat_right, basis_left, basis_right)
    outs = (gradient, moment_one, moment_two, stat_left, stat_right, basis_left, basis_right)
    vm = pl.BlockSpec(memory_space=pltpu.VMEM)
    return pl.pallas_call(
        kernel,
        out_shape=[jax.ShapeDtypeStruct(a.shape, a.dtype) for a in outs],
        in_specs=[vm] * 7,
        out_specs=[vm] * 7,
        scratch_shapes=[pltpu.VMEM(shape, dtype) for shape, dtype in BUFFERS.values()]
        + [
            pltpu.SemaphoreType.DMA((SEMS,)),
            pltpu.SemaphoreType.DMA((SEMS,)),
            pltpu.SemaphoreType.DMA((16,)),
        ],
        compiler_params=pltpu.CompilerParams(
            collective_id=0, has_side_effects=True, vmem_limit_bytes=60 * 2**20
        ),
        name="step",
    )(*args)


def solution(mesh):
    both, row = P("shard", "tensor"), P("shard", None)
    return jax.shard_map(
        local,
        mesh=mesh,
        in_specs=(both, both, both, row, both, row, both),
        out_specs=(both, both, both, row, both, row, both),
        check_vma=False,
    )
```

time: 236 us -> 163 us (0.69)
  Pallas kernels: 195 us -> 155 us
  matrix products: 21.9 us -> 0 us
  other arithmetic: 7.09 us -> 0 us
    pallas_call x9 -> x1, Pallas kernels: 195 us -> 155 us  [local(): pl.pallas_call(kernel, out_shape=[jax.ShapeDtypeStruct(a.shape, a.dtype)...]
    dot_general x13 -> x0, matrix products: 21.9 us -> none  [the longest x11 19.8 us: dot(): return jnp.dot(a, b, preferred_element_type=F32)]
    convert_element_type x5 -> x0, other arithmetic: 3.78 us -> none  [the longest x1 1.79 us: local(): wb = whole.astype(BF)]
    reduce_sum x4 -> x0, other arithmetic: 3.1 us -> none  [the longest x1 1.21 us: local(): squares = jnp.sum(jnp.square(power_rows.astype(F32)))]
    reshape x2 -> x0, local copies, waits for them, and re-layouts: 2.89 us -> none  [local(): back_terms = back_terms.reshape(rows_left, 4, 2, -1).transpose(2, 1, 0, 3)]
    unnamed x25 -> x17, local copies, waits for them, and re-layouts: 5.17 us -> 7.04 us
where the time goes in v2:
time: 163 us
  Pallas kernels  155 us (95%)
  local copies, waits for them, and re-layouts  7.04 us (4%)
    pallas_call x1, Pallas kernels, local(): pl.pallas_call(kernel, out_shape=[jax.ShapeDtypeStruct(a.shape, a.dtype)...  155 us
    unnamed x17, local copies, waits for them, and re-layouts  7.04 us

profile of v2, /device:TPU:0, one launch (start us, length us, event | category | flops | bytes accessed | tf_op | source)
XLA Modules:
  0.0 162.6 jit_solution(9500578074776788863)
XLA Ops:
  0.6 154.9 %step.1 = (bf16[48,384]{1,0:T(8,128)(2,1)}, f32[48,384]{1,0:T(8,128)}, f32[48,384]{1,0:T(8,128)}, f32[48,768]{1,0:T(8,128)}, f32[192,384]{1,0:T(8,128)}, /*index=5*/f32[48,768]{1,0:T(8,128)}, f32[192,384]{1,0:T(8,128)}) custom-call(bf16[48,384]{1,0:T(8,128)(2,1)} %refs_0_.1, f32[48,384]{1,0:T(8,128)} %refs_1_.1, f32[48,384]{1,0:T(8,128)} %refs_2_.1, ...), custom_call_target="tpu_custom_call" | custom-call | tf_op jit(solution)/shard_map/step/pallas_call | solution.py:707
  155.5 0.0 copy-start.4
  155.5 0.0 copy-start.3
  155.5 1.4 copy.21
  157.0 0.0 copy-start.1
  157.0 1.6 copy.22
  158.5 0.0 copy-done.4
  158.5 0.6 copy.23
  159.2 0.0 copy-done.3
  159.2 0.7 copy.24
  159.8 0.0 copy-done.1
  159.8 0.0 copy-start.2
  159.8 0.7 copy.25
  160.5 0.3 copy-done.2
  160.9 0.0 copy-start
  160.9 0.7 copy.26
  161.5 0.4 copy-done
  161.9 0.7 copy.27
Async XLA Ops:
  155.5 3.0 %copy-start.4 = (f32[48,384]{1,0:T(8,128)S(1)}, f32[48,384]{1,0:T(8,128)}, u32[]{:S(2)}) copy-start(f32[48,384]{1,0:T(8,128)} %get-tuple-element.16) | copy-start | bytes 221188
  155.5 3.6 %copy-start.3 = (f32[48,768]{1,0:T(8,128)S(1)}, f32[48,768]{1,0:T(8,128)}, u32[]{:S(2)}) copy-start(f32[48,768]{1,0:T(8,128)} %get-tuple-element.17) | copy-start | bytes 442372
  157.0 2.9 %copy-start.1 = (f32[192,384]{1,0:T(8,128)S(1)}, f32[192,384]{1,0:T(8,128)}, u32[]{:S(2)}) copy-start(f32[192,384]{1,0:T(8,128)} %get-tuple-element.18) | copy-start | bytes 884740
  159.8 1.0 copy-start.2
  160.9 1.0 copy-start

commit v3 on v2

--- a/solution.py
+++ b/solution.py
@@ -171,33 +171,36 @@
 
 
 class TensorGather:
-    def __init__(self, net, src, buf):
-        self.net, self.src, self.buf = net, src, buf
+    def __init__(self, net, src, buf, wide=True):
+        self.net, self.src, self.buf, self.wide = net, src, buf, wide
         rows = src.shape[0]
         self.cut = (0, rows // 32 * 16, rows)
 
     def view(self, dy, other, lo, hi):
-        n, rows = self.net, self.src.shape[0]
+        n, (rows, cols) = self.net, self.src.shape
         slot = (n.y + dy) % 4 * 2 + ((1 - n.c) if other else n.c)
+        if self.wide:
+            return self.buf.at[pl.ds(lo, hi - lo), pl.ds(pl.multiple_of(slot * cols, 128), cols)]
         return self.buf.at[pl.ds(pl.multiple_of(slot * rows + lo, 16), hi - lo), :]
 
     def start(self):
         n = self.net
-        hi = self.cut[2]
-        self.a = {
-            sgn: n.send(self.src, self.view(0, 0, 0, hi), self.view(-sgn, 0, 0, hi), "+y" if sgn > 0 else "-y")
-            for sgn in (1, -1)
-        }
-        self.sib = [n.send(self.src, self.view(0, 0, 0, hi), self.view(0, 1, 0, hi), "c")]
+        lo, mid, hi = self.cut
+        own = lambda a, b: self.src.at[pl.ds(a, b - a), :]
+        put = lambda a, b, sgn: n.send(
+            own(a, b), self.view(0, 0, a, b), self.view(-sgn, 0, a, b), "+y" if sgn > 0 else "-y"
+        )
+        self.a = {1: put(lo, mid, 1), -1: put(mid, hi, -1)}
+        self.rest = {1: put(mid, hi, 1), -1: put(lo, mid, -1)}
+        self.sib = [n.send(self.src, self.view(0, 0, lo, hi), self.view(0, 1, lo, hi), "c")]
 
     def local(self, sem):
-        n = self.net
         self.mine = pltpu.make_async_copy(self.src, self.view(0, 0, 0, self.src.shape[0]), sem)
         self.mine.start()
 
-    def pair(self, dy):
-        n, hi = self.net, self.cut[2]
-        self.sib.append(n.send(self.view(dy, 0, 0, hi), self.view(dy, 0, 0, hi), self.view(dy, 1, 0, hi), "c"))
+    def pair(self, dy, lo, hi):
+        n = self.net
+        self.sib.append(n.send(self.view(dy, 0, lo, hi), self.view(dy, 0, lo, hi), self.view(dy, 1, lo, hi), "c"))
 
     def step1(self):
         n = self.net
@@ -206,15 +209,17 @@
         for sgn in (1, -1):
             self.a[sgn].recv()
             a, b = (lo, mid) if sgn > 0 else (mid, hi)
-            self.aa.append(
-                n.send(self.view(-sgn, 0, a, b), self.view(-sgn, 0, a, b), self.view(2, 0, a, b), "+y" if sgn > 0 else "-y")
-            )
-            self.pair(-sgn)
+            v = self.view(-sgn, 0, a, b)
+            self.aa.append(n.send(v, v, self.view(2, 0, a, b), "+y" if sgn > 0 else "-y"))
 
     def step2(self):
-        for m in self.aa:
+        lo, mid, hi = self.cut
+        for sgn in (1, -1):
+            self.rest[sgn].recv()
+            self.pair(-sgn, lo, hi)
+        for m, (a, b) in zip(self.aa, ((lo, mid), (mid, hi))):
             m.recv()
-        self.pair(2)
+            self.pair(2, a, b)
 
     def finish(self):
         for m in self.sib:
@@ -256,16 +261,20 @@
     def __init__(self, net, src, dst, lsem):
         self.net, self.src, self.dst, self.lsem = net, src, dst, lsem
         self.k = net.count
-        net.count += 5
+        net.count += 8
         self.dy = (net.y - net.z + 4) % 4
         self.main = net.c == net.x // 2
-        self.rows = src.shape[0]
-
-    def msg(self, j, a, lo, hi, d):
+        h = src.shape[0] // 2
+        lo, hi = pl.ds(0, h), pl.ds(h, h)
+        self.kinds = [(lo, "+y"), (hi, "+y"), (hi, "-y"), (lo, "-y"), (lo, "+y"), (hi, "-y"), (lo, "c"), (hi, "c")]
+
+    def msg(self, j, a=None):
         n = self.net
+        cut, d = self.kinds[j]
+        a = self.dst if a is None else a
         return pltpu.make_async_remote_copy(
-            src_ref=a.at[pl.ds(lo, hi - lo), :],
-            dst_ref=self.dst.at[pl.ds(lo, hi - lo), :],
+            src_ref=a.at[cut, :],
+            dst_ref=self.dst.at[cut, :],
             send_sem=n.send_sem.at[self.k + j],
             recv_sem=n.recv_sem.at[self.k + j],
             device_id=n.nbr(d),
@@ -276,60 +285,60 @@
         return pl.when(jnp.logical_and(self.main, self.dy == dy))
 
     def start(self):
-        r = self.rows
-
         @self.at(0)
         def _():
-            self.msg(0, self.src, 0, r, "+y").start()
-            self.msg(1, self.src, 0, r, "-y").start()
-            self.msg(4, self.src, 0, r, "c").start()
+            for j in (0, 2, 1, 3, 6, 7):
+                self.msg(j, self.src).start()
             pltpu.make_async_copy(self.src, self.dst, self.lsem).start()
 
     def middle(self):
-        r, h = self.rows, self.rows // 2
-
-        @self.at(1)
-        def _():
-            self.msg(0, self.dst, 0, r, "+y").wait_recv()
-            self.msg(2, self.dst, 0, h, "+y").start()
-            self.msg(4, self.dst, 0, r, "c").start()
-
-        @self.at(3)
-        def _():
-            self.msg(1, self.dst, 0, r, "-y").wait_recv()
-            self.msg(3, self.dst, h, r, "-y").start()
-            self.msg(4, self.dst, 0, r, "c").start()
+        for dy, j, onward, half in ((1, 0, 4, 6), (3, 2, 5, 7)):
+
+            @self.at(dy)
+            def _(j=j, onward=onward, half=half):
+                self.msg(j).wait_recv()
+                self.msg(onward).start()
+                self.msg(half).start()
 
     def finish(self):
-        r, h = self.rows, self.rows // 2
+        for dy, j, half in ((1, 1, 7), (3, 3, 6)):
+
+            @self.at(dy)
+            def _(j=j, half=half):
+                self.msg(j).wait_recv()
+                self.msg(half).start()
 
         @self.at(2)
         def _():
-            self.msg(2, self.dst, 0, h, "+y").wait_recv()
-            self.msg(3, self.dst, h, r, "-y").wait_recv()
-            self.msg(4, self.dst, 0, r, "c").start()
+            for j, half in ((4, 6), (5, 7)):
+                self.msg(j).wait_recv()
+                self.msg(half).start()
 
         @pl.when(jnp.logical_not(self.main))
         def _():
-            self.msg(4, self.dst, 0, r, "c").wait_recv()
+            self.msg(6).wait_recv()
+            self.msg(7).wait_recv()
 
         @self.at(0)
         def _():
             pltpu.make_async_copy(self.src, self.dst, self.lsem).wait()
-            self.msg(0, self.src, 0, r, "+y").wait_send()
-            self.msg(1, self.src, 0, r, "-y").wait_send()
-
-        @self.at(1)
+
+    def drain(self):
+        @self.at(0)
         def _():
-            self.msg(2, self.dst, 0, h, "+y").wait_send()
-
-        @self.at(3)
-        def _():
-            self.msg(3, self.dst, h, r, "-y").wait_send()
+            for j in range(4):
+                self.msg(j, self.src).wait_send()
+
+        for dy, onward in ((1, 4), (3, 5)):
+
+            @self.at(dy)
+            def _(onward=onward):
+                self.msg(onward).wait_send()
 
         @pl.when(self.main)
         def _():
-            self.msg(4, self.dst, 0, r, "c").wait_send()
+            self.msg(6).wait_send()
+            self.msg(7).wait_send()
 
 
 def plane_scatter(net, part, out, f1, f2, q, g1, g2):
@@ -349,8 +358,9 @@
             return view.at[pl.ds(2 * k, 2)]
 
         stages.append(RingScatter(net, "zx"[i], pick, half, [f1.at[i, 0], f1.at[i, 1]], [f2.at[i, 0], f2.at[i, 1]]))
-    for r in stages:
-        r.start()
+    stages[0].start()
+    yield
+    stages[1].start()
     yield
     for r in stages:
         r.middle()
@@ -410,19 +420,7 @@
     return lax.dot_general(a, b, (((1,), (1,)), ((), ())), preferred_element_type=F32)
 
 
-def rows_dot(blocks, cols, acc):
-    rows, width = acc.shape[0], blocks.shape[1]
-    acc[...] = jnp.zeros_like(acc)
-
-    def step(j, carry):
-        a = blocks[pl.ds(pl.multiple_of(j * rows, 16), rows), :]
-        acc[...] += dot(a, cols[pl.ds(pl.multiple_of(j * width, 16), width), :])
-        return carry
-
-    lax.fori_loop(0, 8, step, 0)
-
-
-SEMS = 430
+SEMS = 343
 ROWS, COLS, LROWS = FF // 16, FF // 8, D // 16
 BUFFERS = dict(
     lq=((LROWS, D), BF),
@@ -435,13 +433,12 @@
     lterms=((LROWS, D), BF),
     lparts=((8 * LROWS, D), BF),
     half_all=((D, COLS), BF),
-    half_rows=((8 * LROWS, COLS), BF),
+    half_rows=((LROWS, FF), BF),
     s_b=((ROWS, COLS), BF),
-    s_rows=((8 * ROWS, COLS), BF),
+    s_rows=((ROWS, FF), BF),
     p=((ROWS, COLS), F32),
     p_b=((ROWS, COLS), BF),
-    p_rows=((8 * ROWS, COLS), BF),
-    rot=((LROWS, COLS), F32),
+    p_rows=((ROWS, FF), BF),
     dir_b=((LROWS, COLS), BF),
     dir_cols=((D, COLS), BF),
     pl_own=((LROWS, D), F32),
@@ -460,14 +457,12 @@
     a=((ROWS, COLS), F32),
     a_b=((ROWS, COLS), BF),
     a_cols=((FF, COLS), BF),
-    a_rows=((8 * ROWS, COLS), BF),
-    t=((ROWS, COLS), F32),
-    t_b=((ROWS, COLS), BF),
-    t_cols=((FF, COLS), BF),
-    t_rows=((8 * ROWS, COLS), BF),
-    w=((ROWS, COLS), F32),
-    w_b=((ROWS, COLS), BF),
-    w_cols=((FF, COLS), BF),
+    y1_b=((ROWS, COLS), BF),
+    y1_rows=((ROWS, FF), BF),
+    y2_b=((ROWS, COLS), BF),
+    y2_rows=((ROWS, FF), BF),
+    y3_b=((ROWS, COLS), BF),
+    y3_rows=((ROWS, FF), BF),
     upart=((2, 4, LROWS, COLS), BF),
     u0=((4, LROWS, COLS), BF),
     uq=((4, LROWS, COLS), BF),
@@ -478,13 +473,18 @@
 
 
 def kernel(*refs):
-    grad, m1, m2, stat_l, stat_r, basis_l, basis_r = refs[:7]
     update, new_m1, new_m2, new_sl, new_sr, new_bl, new_br = refs[7:14]
     b = dict(zip(BUFFERS, refs[14 : 14 + len(BUFFERS)]))
-    send_sem, recv_sem, lsem = refs[14 + len(BUFFERS) :]
+    send_sem, recv_sem, lsem = refs[14 + len(BUFFERS) : 17 + len(BUFFERS)]
+    inputs = refs[17 + len(BUFFERS) :]
+    grad, m1, m2, stat_l, stat_r, basis_l, basis_r = inputs
+    loads = [pltpu.make_async_copy(refs[k], inputs[k], lsem.at[16 + k]) for k in range(7)]
+    for k in (0, 5, 6, 4, 3, 1, 2):
+        loads[k].start()
     net = Net(send_sem, recv_sem)
     x, s = net.x, net.s
     own_left = pl.ds(pl.multiple_of(s * LROWS, 16), LROWS)
+    lanes = lambda c: pl.ds(pl.multiple_of(c * (D // 2), 128), D // 2)
     locals_used = [0]
 
     def begin(*gathers):
@@ -493,111 +493,121 @@
             g.local(lsem.at[locals_used[0]])
             locals_used[0] += 1
 
-    def shard(src, dst):
-        return ShardGather(net, src if not isinstance(src, str) else b[src], b[dst])
-
-    def tensor(src, dst):
-        return TensorGather(net, b[src], b[dst])
-
+    def swap(ref):
+        mine = ref.at[:, lanes(net.c)]
+        return net.send(mine, mine, ref.at[:, lanes(1 - net.c)], "c")
+
+    loads[5].wait()
     b["lq"][...] = (basis_l[...] * (1.0 / math.sqrt(D))).astype(BF)
+    loads[6].wait()
     b["rq"][...] = (basis_r[...] * (1.0 / math.sqrt(FF))).astype(BF)
+    for k in (0, 4, 3, 1, 2):
+        loads[k].wait()
     net.barrier(NBR)
 
-    g_grad, g_left, g_right = shard(grad, "gcols"), shard("lq", "lall"), shard("rq", "qcols")
-    begin(g_grad, g_left)
+    g_grad = ShardGather(net, grad, b["gcols"])
+    g_left = ShardGather(net, b["lq"].at[:, lanes(net.c)], b["lall"].at[:, lanes(net.c)])
+    g_right = ShardGather(net, b["rq"], b["qcols"])
+    begin(g_grad)
     g_grad.step1()
+    begin(g_left)
+    g_grad.step2()
     g_left.step1()
-    g_grad.step2()
-    g_left.step2()
+    begin(g_right)
     g_grad.step3()
     g_grad.finish()
-    begin(g_right)
     cast = LineBroadcast(net, b["gs_own"], b["gs"], lsem.at[locals_used[0]])
     locals_used[0] += 1
     pick = lax.broadcasted_iota(jnp.int32, (COLS, ROWS), 0) == lax.broadcasted_iota(
         jnp.int32, (COLS, ROWS), 1
     ) + ROWS * (x % 2)
-    gcols = b["gcols"][...]
-    b["gs_own"][...] = dot(gcols, jnp.where(pick, 1.0, 0.0).astype(BF)).astype(BF)
+    gcols = b["gcols"]
+    b["gs_own"][...] = dot(gcols[...], jnp.where(pick, 1.0, 0.0).astype(BF)).astype(BF)
     cast.start()
-    b["lterms"][...] = dot_nt(grad[...], gcols).astype(BF)
-    t_lterms = tensor("lterms", "lparts")
+    b["lterms"][...] = dot_nt(grad[...], gcols[...]).astype(BF)
+    t_lterms = TensorGather(net, b["lterms"], b["lparts"], wide=False)
     begin(t_lterms)
-    g_left.step3()
+    g_left.step2()
     g_right.step1()
     cast.middle()
+    g_left.step3()
+    cast.finish()
+
+    new_sr[...] = beta * stat_r[...] + ((1.0 - beta) / D) * dot_tn(b["gs"][...], gcols[...])
+    b["s_b"][...] = new_sr[...].astype(BF)
+    t_stat = TensorGather(net, b["s_b"], b["s_rows"])
+    begin(t_stat)
     g_left.finish()
-    b["half_all"][...] = dot_tn(b["lall"][...], gcols).astype(BF)
+    left_swap = swap(b["lall"])
     g_right.step2()
-    cast.finish()
-
-    new_sr[...] = beta * stat_r[...] + ((1.0 - beta) / D) * dot_tn(b["gs"][...], gcols)
-    b["s_b"][...] = new_sr[...].astype(BF)
-    t_stat = tensor("s_b", "s_rows")
-    begin(t_stat)
+    t_stat.step1()
+    t_lterms.step1()
+    left_swap.recv()
+    b["half_all"][...] = dot_tn(b["lall"][...], gcols[...]).astype(BF)
     t_half = TensorGather(net, b["half_all"].at[own_left, :], b["half_rows"])
     begin(t_half)
-    t_lterms.step1()
     g_right.step3()
-    t_stat.step1()
+    t_stat.step2()
+    t_lterms.step2()
     t_half.step1()
-    t_lterms.step2()
-    t_stat.step2()
-    t_half.step2()
     g_right.finish()
     t_stat.finish()
-    rows_dot(b["s_rows"], b["qcols"], b["p"])
+    b["p"][...] = dot(b["s_rows"][...], b["qcols"][...])
     b["p_b"][...] = b["p"][...].astype(BF)
-    t_power = tensor("p_b", "p_rows")
+    t_power = TensorGather(net, b["p_b"], b["p_rows"])
     begin(t_power)
 
+    t_half.step2()
     t_lterms.finish()
-    t_half.finish()
-    rows_dot(b["half_rows"], b["qcols"], b["rot"])
-    rot = b["rot"][...]
-    first = beta * m1[...] + (1.0 - beta) * rot
-    second = beta * m2[...] + (1.0 - beta) * (rot * rot)
-    new_m1[...] = first
-    new_m2[...] = second
-    b["dir_b"][...] = ((first / correction) / (jnp.sqrt(second / correction) + adam_eps)).astype(BF)
-    g_dir = shard("dir_b", "dir_cols")
-    begin(g_dir)
     gram = b["lparts"][pl.ds(0, LROWS), :].astype(F32)
     for j in range(1, 8):
         gram += b["lparts"][pl.ds(j * LROWS, LROWS), :].astype(F32)
     new_sl[...] = beta * stat_l[...] + ((1.0 - beta) / FF) * gram
     b["pl_own"][...] = dot(new_sl[...].astype(BF), b["lall"][...])
     b["pl_b"][...] = b["pl_own"][...].astype(BF)
-    g_pl = shard("pl_b", "pl_all")
+    t_half.finish()
+    rot = dot(b["half_rows"][...], b["qcols"][...])
+    first = beta * m1[...] + (1.0 - beta) * rot
+    second = beta * m2[...] + (1.0 - beta) * (rot * rot)
+    new_m1[...] = first
+    new_m2[...] = second
+    b["dir_b"][...] = ((first / correction) / (jnp.sqrt(second / correction) + adam_eps)).astype(BF)
+    g_dir = ShardGather(net, b["dir_b"], b["dir_cols"])
+    begin(g_dir)
+    g_pl = ShardGather(net, b["pl_b"].at[:, lanes(net.c)], b["pl_all"].at[:, lanes(net.c)])
     begin(g_pl)
     t_power.step1()
     g_dir.step1()
     g_pl.step1()
     t_power.step2()
+    g_dir.step2()
+    g_pl.step2()
     t_power.finish()
+
+    def term(rel):
+        zt = (net.z + rel) % 4
+        v = dot_tn(b["p_rows"][:, pl.ds(pl.multiple_of(zt * D, 128), D)], b["p_b"][...]).astype(BF)
+        b["part"][zt] = v.reshape(4, ROWS, COLS)
+
+    scatter = plane_scatter(net, b["part"], b["a"], b["f1"], b["f2"], b["fq"], b["fg1"], b["fg2"])
+    term(2)
+    next(scatter)
+    for rel in (1, 3, 0):
+        term(rel)
+    next(scatter)
+    g_dir.step3()
+    g_pl.step3()
 
     def squares(j, total):
         v = b["p_rows"][pl.ds(pl.multiple_of(j * 16, 16), 16), :].astype(F32)
-        return total + v * v
-
-    def term(j, carry):
-        v = dot_tn(b["p_rows"][pl.ds(pl.multiple_of(j * ROWS, 16), ROWS), :], b["p_b"][...]).astype(BF)
-        b["part"][j // 2, pl.ds(j % 2 * 2, 2), :, :] = v.reshape(2, ROWS, COLS)
-        return carry
-
-    lax.fori_loop(0, 8, term, 0)
-    scatter = plane_scatter(net, b["part"], b["a"], b["f1"], b["f2"], b["fq"], b["fg1"], b["fg2"])
-    next(scatter)
-    total = lax.fori_loop(0, ROWS // 2, squares, jnp.zeros((16, COLS), F32))
+        return total + jnp.sum(v * v, axis=0, keepdims=True)
+
+    total = lax.fori_loop(0, ROWS // 16, squares, jnp.zeros((1, FF), F32))
     b["tile"][...] = jnp.broadcast_to(jnp.sum(total, keepdims=True), (8, 128))
-    g_tile = shard("tile", "tiles")
+    g_tile = ShardGather(net, b["tile"], b["tiles"])
     begin(g_tile)
-    g_dir.step2()
-    g_pl.step2()
     next(scatter)
     g_tile.step1()
-    g_dir.step3()
-    g_pl.step3()
     next(scatter)
     g_tile.step2()
     next(scatter)
@@ -607,119 +617,112 @@
     g_tile.finish()
     norm = jnp.sum(b["tiles"][...], keepdims=True) / 1024.0
     scale = math.sqrt(FF) / (4.0 * jnp.sqrt(norm))
-    b["a"][...] = b["a"][...] * (scale * scale)
-    b["a_b"][...] = b["a"][...].astype(BF)
-    g_a, t_a = shard("a_b", "a_cols"), tensor("a_b", "a_rows")
-    begin(g_a, t_a)
+    b["a_b"][...] = (b["a"][...] * (scale * scale)).astype(BF)
+    g_a = ShardGather(net, b["a_b"], b["a_cols"])
+    begin(g_a)
 
     g_dir.finish()
+    g_pl.finish()
+    pl_swap = swap(b["pl_all"])
     back = dot(b["lq"][...], b["dir_cols"][...]).astype(BF)
-
-    def back_term(j, carry):
-        v = dot_nt(back, b["qcols"][pl.ds(pl.multiple_of(j * COLS, 16), COLS), :])
-        b["upart"][j % 2, j // 2] = v.astype(BF)
-        return carry
-
-    lax.fori_loop(0, 8, back_term, 0)
+    for j in range(8):
+        b["upart"][j % 2, j // 2] = dot_nt(back, b["qcols"][pl.ds(j * COLS, COLS), :]).astype(BF)
     to_update = line_scatter(net, b["upart"], update, b["u0"], b["uq"], b["u1"], b["u2"])
+    next(to_update)
     g_a.step1()
-    t_a.step1()
     next(to_update)
-    g_a.step2()
-    t_a.step2()
-    next(to_update)
-
-    g_pl.finish()
+
+    pl_swap.recv()
 
     def left_squares(j, total):
         v = b["pl_all"][pl.ds(pl.multiple_of(j * 16, 16), 16), :].astype(F32)
-        return total + v * v
-
-    left_total = lax.fori_loop(0, D // 16, left_squares, jnp.zeros((16, D), F32))
+        return total + jnp.sum(v * v, axis=0, keepdims=True)
+
+    left_total = lax.fori_loop(0, D // 16, left_squares, jnp.zeros((1, D), F32))
     left_scale = math.sqrt(D) / (4.0 * jnp.sqrt(jnp.sum(left_total, keepdims=True)))
 
-    def left_gram(ref, factor):
-        def step(j, carry):
-            cut = pl.ds(pl.multiple_of(j * 128, 128), 128)
+    def left_gram(ref, factor, lo, hi):
+        for j in range(lo, hi):
+            cut = pl.ds(j * 128, 128)
             b["gl"][cut, :] = (dot_tn(ref[:, cut], ref[...]) * factor).astype(BF)
-            return carry
-
-        lax.fori_loop(0, D // 128, step, 0)
-
+
+    left_gram(b["pl_all"], left_scale * left_scale, 0, 6)
+    g_a.step2()
+    next(to_update)
     g_a.step3()
-    left_gram(b["pl_all"], left_scale * left_scale)
-    next(to_update)
     g_a.finish()
-    t_a.finish()
+
+    def mix(rows, factor, add, out, all_rows):
+        v = dot(b[rows][...], b["a_cols"][...])
+        b[out][...] = ((factor * v if factor != 1.0 else v) + add * b["p"][...]).astype(BF)
+        g = TensorGather(net, b[out], b[all_rows])
+        begin(g)
+        return g
+
+    t_y = mix("p_rows", 0.0625, -0.5625, "y1_b", "y1_rows")
     for _ in to_update:
         pass
-
-    rows_dot(b["a_rows"], b["a_cols"], b["t"])
-    b["t_b"][...] = b["t"][...].astype(BF)
-    g_t, t_t = shard("t_b", "t_cols"), tensor("t_b", "t_rows")
-    begin(g_t, t_t)
-
-    def left_step(j, carry):
-        cut = pl.ds(pl.multiple_of(j * 128, 128), 128)
+    t_y.step1()
+    for j in range(3):
+        cut = pl.ds(j * 256, 256)
         v = b["pl_all"][cut, :]
         b["wl"][cut, :] = (left_scale * (1.5 * v.astype(F32) - 0.5 * dot(v, b["gl"][...]))).astype(BF)
-        return carry
-
-    lax.fori_loop(0, D // 128, left_step, 0)
-    b["pl_own"][...] = left_scale * (1.5 * b["pl_own"][...] - 0.5 * dot(b["pl_b"][...], b["gl"][...]))
-    g_t.step1()
-    t_t.step1()
-    g_t.step2()
-    t_t.step2()
-    g_t.step3()
-    t_t.finish()
-
-    def blend(j, carry):
-        cut = pl.ds(pl.multiple_of(j * ROWS, 16), ROWS)
-        v = -0.5625 * b["a_rows"][cut, :].astype(F32) + 0.0625 * b["t_rows"][cut, :].astype(F32)
-        b["t_rows"][cut, :] = v.astype(BF)
-        return carry
-
-    net.drain()
-    lax.fori_loop(0, 8, blend, 0)
-    g_t.finish()
-
-    rows_dot(b["t_rows"], b["t_cols"], b["w"])
-    b["w_b"][...] = (b["w"][...] - 2.4375 * b["a"][...] + 1.6875 * b["t"][...]).astype(BF)
-    g_w = shard("w_b", "w_cols")
-    begin(g_w)
-    left_gram(b["wl"], 1.0)
+    mine = left_scale * (1.5 * b["pl_own"][...] - 0.5 * dot(b["pl_b"][...], b["gl"][...]))
+    b["pl_own"][...] = mine
+    t_y.step2()
+    t_y.finish()
+    t_y = mix("y1_rows", 1.0, 1.6875, "y2_b", "y2_rows")
+    left_gram(b["wl"], 1.0, 0, 3)
+    t_y.step1()
+    left_gram(b["wl"], 1.0, 3, 6)
+    t_y.step2()
+    t_y.finish()
+    t_y = mix("y2_rows", 1.0, -2.4375, "y3_b", "y3_rows")
     mine = b["pl_own"][...]
     new_bl[...] = math.sqrt(D) * (1.5 * mine - 0.5 * dot(mine.astype(BF), b["gl"][...]))
-    g_w.step1()
-    g_w.step2()
-    g_w.step3()
-    g_w.finish()
-    rows_dot(b["p_rows"], b["w_cols"], b["w"])
-    new_br[...] = (math.sqrt(FF) * scale) * (2.25 * b["p"][...] + b["w"][...])
+    t_y.step1()
+    t_y.step2()
+    t_y.finish()
+    v = dot(b["y3_rows"][...], b["a_cols"][...])
+    new_br[...] = (math.sqrt(FF) * scale) * (2.25 * b["p"][...] + v)
+    assert net.count <= SEMS and locals_used[0] <= 16
+    cast.drain()
     net.drain()
+
+
+def emit(*refs):
+    for a, o in zip(refs[:7], refs[7:]):
+        o[...] = a[...]
 
 
 def local(gradient, moment_one, moment_two, stat_left, stat_right, basis_left, basis_right):
     args = (gradient, moment_one, moment_two, stat_left, stat_right, basis_left, basis_right)
-    outs = (gradient, moment_one, moment_two, stat_left, stat_right, basis_left, basis_right)
     vm = pl.BlockSpec(memory_space=pltpu.VMEM)
-    return pl.pallas_call(
+    out = pl.pallas_call(
         kernel,
-        out_shape=[jax.ShapeDtypeStruct(a.shape, a.dtype) for a in outs],
-        in_specs=[vm] * 7,
+        out_shape=[jax.ShapeDtypeStruct(a.shape, a.dtype) for a in args],
+        in_specs=[pl.BlockSpec(memory_space=pl.ANY)] * 7,
         out_specs=[vm] * 7,
         scratch_shapes=[pltpu.VMEM(shape, dtype) for shape, dtype in BUFFERS.values()]
         + [
             pltpu.SemaphoreType.DMA((SEMS,)),
             pltpu.SemaphoreType.DMA((SEMS,)),
-            pltpu.SemaphoreType.DMA((16,)),
-        ],
+            pltpu.SemaphoreType.DMA((23,)),
+        ]
+        + [pltpu.VMEM(a.shape, a.dtype) for a in args],
         compiler_params=pltpu.CompilerParams(
-            collective_id=0, has_side_effects=True, vmem_limit_bytes=60 * 2**20
+            collective_id=0, has_side_effects=True, vmem_limit_bytes=63 * 2**20
         ),
         name="step",
     )(*args)
+    return pl.pallas_call(
+        emit,
+        out_shape=[jax.ShapeDtypeStruct(a.shape, a.dtype) for a in args],
+        in_specs=[vm] * 7,
+        out_specs=[vm] * 7,
+        compiler_params=pltpu.CompilerParams(vmem_limit_bytes=63 * 2**20),
+        name="emit",
+    )(*out)
 
 
 def solution(mesh):

time: 163 us -> 135 us (0.83)
  Pallas kernels: 155 us -> 132 us
  local copies, waits for them, and re-layouts: 7.04 us -> 0 us
    pallas_call x1, Pallas kernels: 155 us -> 130 us  [local(): pl.pallas_call(kernel, out_shape=[jax.ShapeDtypeStruct(a.shape, a.dtype)...]
    unnamed x17 -> x0, local copies, waits for them, and re-layouts: 7.04 us -> none
    pallas_call x0 -> x1, Pallas kernels: none -> 2.27 us  [local(): pl.pallas_call(emit, out_shape=[jax.ShapeDtypeStruct(a.shape, a.dtype) fo...]
where the time goes in v3:
time: 135 us; the launch traced here: 133 us
  Pallas kernels  132 us (98%)
    pallas_call x1, Pallas kernels, local(): pl.pallas_call(kernel, out_shape=[jax.ShapeDtypeStruct(a.shape, a.dtype)...  130 us

profile of v3, /device:TPU:0, one launch (start us, length us, event | category | flops | bytes accessed | tf_op | source)
XLA Modules:
  0.0 133.0 jit_solution(8256054137575563430)
XLA Ops:
  0.6 130.1 %step.1 = (bf16[48,384]{1,0:T(8,128)(2,1)}, f32[48,384]{1,0:T(8,128)}, f32[48,384]{1,0:T(8,128)}, f32[48,768]{1,0:T(8,128)}, f32[192,384]{1,0:T(8,128)}, /*index=5*/f32[48,768]{1,0:T(8,128)}, f32[192,384]{1,0:T(8,128)}) custom-call(bf16[48,384]{1,0:T(8,128)(2,1)} %refs_0_.1, f32[48,384]{1,0:T(8,128)} %refs_1_.1, f32[48,384]{1,0:T(8,128)} %refs_2_.1, ...), custom_call_target="tpu_custom_call" | custom-call | tf_op jit(solution)/shard_map/step/pallas_call | solution.py:701
  130.7 2.3 %emit.1 = (bf16[48,384]{1,0:T(8,128)(2,1)}, f32[48,384]{1,0:T(8,128)}, f32[48,384]{1,0:T(8,128)}, f32[48,768]{1,0:T(8,128)}, f32[192,384]{1,0:T(8,128)}, /*index=5*/f32[48,768]{1,0:T(8,128)}, f32[192,384]{1,0:T(8,128)}) custom-call(bf16[48,384]{1,0:T(8,128)(2,1)} %get-tuple-element.14.refs_0_, f32[48,384]{1,0:T(8,128)} %get-tuple-element.15.refs_1_, ...), custom_call_target="tpu_custom_call" | custom-call | tf_op jit(solution)/shard_map/emit/pallas_call | solution.py:718

commit v4 on v3

--- a/solution.py
+++ b/solution.py
@@ -20,61 +20,82 @@
 
 
 class Move:
-    def __init__(self, copy, landing):
-        self.copy, self.landing = copy, landing
+    def __init__(self, landing):
+        self.landing = landing
 
     def recv(self):
         self.landing.wait_recv()
+
+
+class Slots:
+    def __init__(self, first, count):
+        self.first, self.count, self.used = first, count, 0
+
+    def next(self):
+        self.used += 1
+        assert self.used <= self.count
+        return self.first + self.used - 1
+
+    def again(self):
+        return Slots(self.first, self.count)
 
 
 class Net:
     def __init__(self, send_sem, recv_sem):
         self.send_sem, self.recv_sem = send_sem, recv_sem
         self.count = 0
-        self.sent = []
+        self.taken = 0
+        self.sent = {}
         s, t = lax.axis_index("shard"), lax.axis_index("tensor")
         self.s, self.t = s, t
         self.z, self.x = s // 4, s % 4
         self.y, self.c = t // 2, t % 2
+
+    def take(self, count):
+        self.taken += count
+        return Slots(self.taken - count, count)
 
     def nbr(self, d):
         s, t = self.s, self.t
         z, x, y, c = self.z, self.x, self.y, self.c
         if d == "c":
             return (s, y * 2 + 1 - c)
-        step = 1 if d[0] == "+" else 3
+        step = {"+": 1, "2": 2, "-": 3}[d[0]]
         if d[1] == "x":
             return (z * 4 + (x + step) % 4, t)
         if d[1] == "z":
             return (((z + step) % 4) * 4 + x, t)
         return (s, ((y + step) % 4) * 2 + c)
 
-    def barrier(self, dirs):
+    def greet(self, dirs):
         sem = pltpu.get_barrier_semaphore()
         for d in dirs:
             pl.semaphore_signal(sem, inc=1, device_id=self.nbr(d), device_id_type=MESH)
-        pl.semaphore_wait(sem, len(dirs))
-
-    def send(self, src, dst, landing, d):
-        k = self.count
+
+    def meet(self, dirs):
+        pl.semaphore_wait(pltpu.get_barrier_semaphore(), len(dirs))
+
+    def send(self, src, dst, landing, d, slots):
+        k, r = self.count % POOL, slots.next()
         self.count += 1
+        if k in self.sent:
+            self.sent[k].wait_send()
         mk = lambda a, b: pltpu.make_async_remote_copy(
             src_ref=a,
             dst_ref=b,
             send_sem=self.send_sem.at[k],
-            recv_sem=self.recv_sem.at[k],
+            recv_sem=self.recv_sem.at[r],
             device_id=self.nbr(d),
             device_id_type=MESH,
         )
-        copy = mk(src, dst)
-        copy.start()
-        self.sent.append(copy)
-        return Move(copy, mk(landing, landing))
+        self.sent[k] = mk(src, dst)
+        self.sent[k].start()
+        return Move(mk(landing, landing))
 
     def drain(self):
-        for copy in self.sent:
+        for copy in self.sent.values():
             copy.wait_send()
-        self.sent = []
+        self.sent = {}
 
 
 def cuts(rows):
@@ -87,10 +108,11 @@
 
 
 class ShardGather:
-    def __init__(self, net, src, buf):
-        self.net, self.src, self.buf = net, src, buf
+    def __init__(self, net, src, buf, direct=False, slots=None):
+        self.net, self.src, self.buf, self.direct = net, src, buf, direct
         self.flows = [(i, f) for i, f in enumerate(cuts(src.shape[0])) if f is not None]
         self.m = {}
+        self.slots = slots or net.take(40 if self.flows[-1][0] else 20)
 
     def view(self, blk, lo, hi):
         n, rows = self.net, self.src.shape[0]
@@ -111,7 +133,7 @@
         blk = self.rel(i, first, second)
         lf, ls = (first - sgn, second) if stage == 0 else (first, second - sgn)
         src = self.src.at[pl.ds(lo, hi - lo), :] if own else self.view(blk, lo, hi)
-        self.m[key] = self.net.send(src, self.view(blk, lo, hi), self.view(self.rel(i, lf, ls), lo, hi), d)
+        self.m[key] = self.net.send(src, self.view(blk, lo, hi), self.view(self.rel(i, lf, ls), lo, hi), d, self.slots)
 
     def wait(self, *key):
         if key in self.m:
@@ -122,6 +144,10 @@
         for i, (lo, mid, hi) in self.flows:
             for sgn in (1, -1):
                 self.go(i, 0, sgn, 0, 0, lo, hi, (i, "a", sgn), own=True)
+            if self.direct:
+                src = self.src.at[pl.ds(lo, hi - lo), :]
+                landing = self.view(self.rel(i, 2, 0), lo, hi)
+                self.m[i, "aa", 1] = n.send(src, self.view((0, 0), lo, hi), landing, "2" + self.axes(i)[0], self.slots)
         for i, (lo, mid, hi) in self.flows:
             for sgn in (1, -1):
                 self.go(i, 1, sgn, 0, 0, lo, hi, (i, "b", 0, sgn), own=True)
@@ -146,7 +172,8 @@
             for sgn in (1, -1):
                 self.wait(i, "a", sgn)
                 a, b = (lo, mid) if sgn > 0 else (mid, hi)
-                self.go(i, 0, sgn, -sgn, 0, a, b, (i, "aa", sgn))
+                if not self.direct:
+                    self.go(i, 0, sgn, -sgn, 0, a, b, (i, "aa", sgn))
                 self.second(i, -sgn, lo, hi)
 
     def step2(self):
@@ -171,8 +198,9 @@
 
 
 class TensorGather:
-    def __init__(self, net, src, buf, wide=True):
+    def __init__(self, net, src, buf, wide=True, slots=None):
         self.net, self.src, self.buf, self.wide = net, src, buf, wide
+        self.slots = slots or net.take(11)
         rows = src.shape[0]
         self.cut = (0, rows // 32 * 16, rows)
 
@@ -188,11 +216,11 @@
         lo, mid, hi = self.cut
         own = lambda a, b: self.src.at[pl.ds(a, b - a), :]
         put = lambda a, b, sgn: n.send(
-            own(a, b), self.view(0, 0, a, b), self.view(-sgn, 0, a, b), "+y" if sgn > 0 else "-y"
+            own(a, b), self.view(0, 0, a, b), self.view(-sgn, 0, a, b), "+y" if sgn > 0 else "-y", self.slots
         )
         self.a = {1: put(lo, mid, 1), -1: put(mid, hi, -1)}
         self.rest = {1: put(mid, hi, 1), -1: put(lo, mid, -1)}
-        self.sib = [n.send(self.src, self.view(0, 0, lo, hi), self.view(0, 1, lo, hi), "c")]
+        self.sib = [n.send(self.src, self.view(0, 0, lo, hi), self.view(0, 1, lo, hi), "c", self.slots)]
 
     def local(self, sem):
         self.mine = pltpu.make_async_copy(self.src, self.view(0, 0, 0, self.src.shape[0]), sem)
@@ -200,7 +228,7 @@
 
     def pair(self, dy, lo, hi):
         n = self.net
-        self.sib.append(n.send(self.view(dy, 0, lo, hi), self.view(dy, 0, lo, hi), self.view(dy, 1, lo, hi), "c"))
+        self.sib.append(n.send(self.view(dy, 0, lo, hi), self.view(dy, 0, lo, hi), self.view(dy, 1, lo, hi), "c", self.slots))
 
     def step1(self):
         n = self.net
@@ -210,7 +238,7 @@
             self.a[sgn].recv()
             a, b = (lo, mid) if sgn > 0 else (mid, hi)
             v = self.view(-sgn, 0, a, b)
-            self.aa.append(n.send(v, v, self.view(2, 0, a, b), "+y" if sgn > 0 else "-y"))
+            self.aa.append(n.send(v, v, self.view(2, 0, a, b), "+y" if sgn > 0 else "-y", self.slots))
 
     def step2(self):
         lo, mid, hi = self.cut
@@ -235,20 +263,28 @@
     def __init__(self, net, axis, pick, half, first, second):
         self.net, self.axis, self.pick, self.half = net, axis, pick, half
         self.first, self.second = first, second
+        self.slots = net.take(6)
 
     def start(self):
         n = self.net
-        self.one = [
-            n.send(self.half(self.pick(2), h), self.first[h], self.first[h], ("+", "-")[h] + self.axis) for h in (0, 1)
-        ]
+        way = lambda h: ("+", "-")[h] + self.axis
+        self.one = [n.send(self.half(self.pick(2), h), self.first[h], self.first[h], way(h), self.slots) for h in (0, 1)]
+
+    def near(self):
+        n = self.net
+        way = lambda h: ("+", "-")[h] + self.axis
+        self.two = []
+        for h, rel in ((0, 1), (1, -1)):
+            dst = self.half(self.second[h], 1 - h)
+            self.two.append(n.send(self.half(self.pick(rel), 1 - h), dst, dst, way(h), self.slots))
 
     def middle(self):
         n = self.net
-        self.two = []
         for h, rel in ((0, 1), (1, -1)):
             self.one[h].recv()
             add_into(self.half(self.pick(rel), h), self.first[h])
-            self.two.append(n.send(self.pick(rel), self.second[h], self.second[h], ("+", "-")[h] + self.axis))
+            dst = self.half(self.second[h], h)
+            self.two.append(n.send(self.half(self.pick(rel), h), dst, dst, ("+", "-")[h] + self.axis, self.slots))
 
     def total(self):
         for m in self.two:
@@ -260,8 +296,7 @@
 class LineBroadcast:
     def __init__(self, net, src, dst, lsem):
         self.net, self.src, self.dst, self.lsem = net, src, dst, lsem
-        self.k = net.count
-        net.count += 8
+        self.slots = net.take(8)
         self.dy = (net.y - net.z + 4) % 4
         self.main = net.c == net.x // 2
         h = src.shape[0] // 2
@@ -275,8 +310,8 @@
         return pltpu.make_async_remote_copy(
             src_ref=a.at[cut, :],
             dst_ref=self.dst.at[cut, :],
-            send_sem=n.send_sem.at[self.k + j],
-            recv_sem=n.recv_sem.at[self.k + j],
+            send_sem=n.send_sem.at[POOL + j],
+            recv_sem=n.recv_sem.at[self.slots.first + j],
             device_id=n.nbr(d),
             device_id_type=MESH,
         )
@@ -360,7 +395,10 @@
         stages.append(RingScatter(net, "zx"[i], pick, half, [f1.at[i, 0], f1.at[i, 1]], [f2.at[i, 0], f2.at[i, 1]]))
     stages[0].start()
     yield
+    stages[0].near()
+    yield
     stages[1].start()
+    stages[1].near()
     yield
     for r in stages:
         r.middle()
@@ -377,6 +415,7 @@
 
         later.append(RingScatter(net, "xz"[i], pick, half, [g1.at[i, 0], g1.at[i, 1]], [g2.at[i, 0], g2.at[i, 1]]))
         later[-1].start()
+        later[-1].near()
     yield
     for r in later:
         r.middle()
@@ -388,7 +427,7 @@
 def line_scatter(net, part, out, g0, q, g1, g2):
     y, c = net.y, net.c
     rows = part.shape[2]
-    m = net.send(part.at[1 - c], g0, g0, "c")
+    m = net.send(part.at[1 - c], g0, g0, "c", net.take(1))
     yield
     m.recv()
     q[...] = (part[c].astype(F32) + g0[...].astype(F32)).astype(q.dtype)
@@ -402,6 +441,7 @@
 
     ring = RingScatter(net, "y", pick, half, [g1.at[pl.ds(0, cut)], g1.at[pl.ds(cut, rows - cut)]], [g2.at[0], g2.at[1]])
     ring.start()
+    ring.near()
     yield
     ring.middle()
     yield
@@ -420,7 +460,7 @@
     return lax.dot_general(a, b, (((1,), (1,)), ((), ())), preferred_element_type=F32)
 
 
-SEMS = 343
+SEMS, POOL = 268, 72
 ROWS, COLS, LROWS = FF // 16, FF // 8, D // 16
 BUFFERS = dict(
     lq=((LROWS, D), BF),
@@ -469,14 +509,15 @@
     u1=((LROWS, COLS), BF),
     u2=((2, LROWS, COLS), BF),
 )
-NBR = ("+x", "-x", "+z", "-z", "+y", "-y", "c")
+NBR = ("+x", "-x", "2x", "+z", "-z", "2z", "+y", "-y", "c")
 
 
 def kernel(*refs):
-    update, new_m1, new_m2, new_sl, new_sr, new_bl, new_br = refs[7:14]
     b = dict(zip(BUFFERS, refs[14 : 14 + len(BUFFERS)]))
     send_sem, recv_sem, lsem = refs[14 + len(BUFFERS) : 17 + len(BUFFERS)]
-    inputs = refs[17 + len(BUFFERS) :]
+    inputs, outputs = refs[17 + len(BUFFERS) : 24 + len(BUFFERS)], refs[24 + len(BUFFERS) :]
+    update, new_m1, new_m2, new_sl, new_sr, new_bl, new_br = outputs
+    stores = [pltpu.make_async_copy(outputs[k], refs[7 + k], lsem.at[23 + k]) for k in range(7)]
     grad, m1, m2, stat_l, stat_r, basis_l, basis_r = inputs
     loads = [pltpu.make_async_copy(refs[k], inputs[k], lsem.at[16 + k]) for k in range(7)]
     for k in (0, 5, 6, 4, 3, 1, 2):
@@ -495,26 +536,29 @@
 
     def swap(ref):
         mine = ref.at[:, lanes(net.c)]
-        return net.send(mine, mine, ref.at[:, lanes(1 - net.c)], "c")
-
+        return net.send(mine, mine, ref.at[:, lanes(1 - net.c)], "c", net.take(1))
+
+    net.greet(NBR)
+    loads[0].wait()
+    net.meet(NBR)
+
+    g_grad = ShardGather(net, grad, b["gcols"], direct=True)
+    begin(g_grad)
     loads[5].wait()
     b["lq"][...] = (basis_l[...] * (1.0 / math.sqrt(D))).astype(BF)
     loads[6].wait()
     b["rq"][...] = (basis_r[...] * (1.0 / math.sqrt(FF))).astype(BF)
-    for k in (0, 4, 3, 1, 2):
+    for k in (4, 3, 1, 2):
         loads[k].wait()
-    net.barrier(NBR)
-
-    g_grad = ShardGather(net, grad, b["gcols"])
     g_left = ShardGather(net, b["lq"].at[:, lanes(net.c)], b["lall"].at[:, lanes(net.c)])
     g_right = ShardGather(net, b["rq"], b["qcols"])
-    begin(g_grad)
     g_grad.step1()
     begin(g_left)
     g_grad.step2()
     g_left.step1()
+    g_grad.step3()
     begin(g_right)
-    g_grad.step3()
+    g_left.step2()
     g_grad.finish()
     cast = LineBroadcast(net, b["gs_own"], b["gs"], lsem.at[locals_used[0]])
     locals_used[0] += 1
@@ -527,37 +571,24 @@
     b["lterms"][...] = dot_nt(grad[...], gcols[...]).astype(BF)
     t_lterms = TensorGather(net, b["lterms"], b["lparts"], wide=False)
     begin(t_lterms)
-    g_left.step2()
     g_right.step1()
     cast.middle()
     g_left.step3()
+    t_lterms.step1()
+    g_right.step2()
     cast.finish()
 
     new_sr[...] = beta * stat_r[...] + ((1.0 - beta) / D) * dot_tn(b["gs"][...], gcols[...])
     b["s_b"][...] = new_sr[...].astype(BF)
     t_stat = TensorGather(net, b["s_b"], b["s_rows"])
     begin(t_stat)
+    stores[4].start()
     g_left.finish()
     left_swap = swap(b["lall"])
-    g_right.step2()
+    t_lterms.step2()
+    g_right.step3()
     t_stat.step1()
-    t_lterms.step1()
     left_swap.recv()
-    b["half_all"][...] = dot_tn(b["lall"][...], gcols[...]).astype(BF)
-    t_half = TensorGather(net, b["half_all"].at[own_left, :], b["half_rows"])
-    begin(t_half)
-    g_right.step3()
-    t_stat.step2()
-    t_lterms.step2()
-    t_half.step1()
-    g_right.finish()
-    t_stat.finish()
-    b["p"][...] = dot(b["s_rows"][...], b["qcols"][...])
-    b["p_b"][...] = b["p"][...].astype(BF)
-    t_power = TensorGather(net, b["p_b"], b["p_rows"])
-    begin(t_power)
-
-    t_half.step2()
     t_lterms.finish()
     gram = b["lparts"][pl.ds(0, LROWS), :].astype(F32)
     for j in range(1, 8):
@@ -565,161 +596,189 @@
     new_sl[...] = beta * stat_l[...] + ((1.0 - beta) / FF) * gram
     b["pl_own"][...] = dot(new_sl[...].astype(BF), b["lall"][...])
     b["pl_b"][...] = b["pl_own"][...].astype(BF)
+    g_pl = ShardGather(net, b["pl_b"].at[:, lanes(net.c)], b["pl_all"].at[:, lanes(net.c)])
+    begin(g_pl)
+    stores[3].start()
+    b["half_all"][...] = dot_tn(b["lall"][...], gcols[...]).astype(BF)
+    t_half = TensorGather(net, b["half_all"].at[own_left, :], b["half_rows"])
+    t_stat.step2()
+    begin(t_half)
+    g_right.finish()
+    t_stat.finish()
+    b["p"][...] = dot(b["s_rows"][...], b["qcols"][...])
+    b["p_b"][...] = b["p"][...].astype(BF)
+    t_power = TensorGather(net, b["p_b"], b["p_rows"])
+    begin(t_power)
+    g_pl.step1()
+    t_half.step1()
+    t_power.step1()
+    g_pl.step2()
+    t_half.step2()
+    t_power.step2()
+    g_pl.step3()
+    t_power.finish()
+
+    def term(rel):
+        zt = (net.z + rel) % 4
+        v = dot_tn(b["p_rows"][:, pl.ds(pl.multiple_of(zt * D, 128), D)], b["p_b"][...]).astype(BF)
+        b["part"][zt] = v.reshape(4, ROWS, COLS)
+
+    scatter = plane_scatter(net, b["part"], b["a"], b["f1"], b["f2"], b["fq"], b["fg1"], b["fg2"])
+    term(2)
+    next(scatter)
+    term(1)
+    term(3)
+    next(scatter)
+    term(0)
+    next(scatter)
+
+    def squares(j, total):
+        v = b["p_rows"][pl.ds(pl.multiple_of(j * 16, 16), 16), :].astype(F32)
+        return total + jnp.sum(v * v, axis=0, keepdims=True)
+
+    total = lax.fori_loop(0, ROWS // 16, squares, jnp.zeros((1, FF), F32))
+    b["tile"][...] = jnp.broadcast_to(jnp.sum(total, keepdims=True), (8, 128))
+    g_tile = ShardGather(net, b["tile"], b["tiles"])
+    begin(g_tile)
     t_half.finish()
     rot = dot(b["half_rows"][...], b["qcols"][...])
     first = beta * m1[...] + (1.0 - beta) * rot
     second = beta * m2[...] + (1.0 - beta) * (rot * rot)
     new_m1[...] = first
     new_m2[...] = second
+    stores[1].start()
+    stores[2].start()
     b["dir_b"][...] = ((first / correction) / (jnp.sqrt(second / correction) + adam_eps)).astype(BF)
-    g_dir = ShardGather(net, b["dir_b"], b["dir_cols"])
-    begin(g_dir)
-    g_pl = ShardGather(net, b["pl_b"].at[:, lanes(net.c)], b["pl_all"].at[:, lanes(net.c)])
-    begin(g_pl)
-    t_power.step1()
-    g_dir.step1()
-    g_pl.step1()
-    t_power.step2()
-    g_dir.step2()
-    g_pl.step2()
-    t_power.finish()
-
-    def term(rel):
-        zt = (net.z + rel) % 4
-        v = dot_tn(b["p_rows"][:, pl.ds(pl.multiple_of(zt * D, 128), D)], b["p_b"][...]).astype(BF)
-        b["part"][zt] = v.reshape(4, ROWS, COLS)
-
-    scatter = plane_scatter(net, b["part"], b["a"], b["f1"], b["f2"], b["fq"], b["fg1"], b["fg2"])
-    term(2)
     next(scatter)
-    for rel in (1, 3, 0):
-        term(rel)
-    next(scatter)
-    g_dir.step3()
-    g_pl.step3()
-
-    def squares(j, total):
-        v = b["p_rows"][pl.ds(pl.multiple_of(j * 16, 16), 16), :].astype(F32)
+    g_pl.finish()
+    pl_swap = swap(b["pl_all"])
+    pl_swap.recv()
+
+    def left_squares(j, total):
+        v = b["pl_all"][pl.ds(pl.multiple_of(j * 16, 16), 16), :].astype(F32)
         return total + jnp.sum(v * v, axis=0, keepdims=True)
 
-    total = lax.fori_loop(0, ROWS // 16, squares, jnp.zeros((1, FF), F32))
-    b["tile"][...] = jnp.broadcast_to(jnp.sum(total, keepdims=True), (8, 128))
-    g_tile = ShardGather(net, b["tile"], b["tiles"])
-    begin(g_tile)
-    next(scatter)
+    def left_gram(ref, factor, lo, hi):
+        for j in range(lo, hi):
+            cut = pl.ds(j * 128, 128)
+            b["gl"][cut, :] = (dot_tn(ref[:, cut], ref[...]) * factor).astype(BF)
+
+    left_total = lax.fori_loop(0, D // 16, left_squares, jnp.zeros((1, D), F32))
+    left_scale = math.sqrt(D) / (4.0 * jnp.sqrt(jnp.sum(left_total, keepdims=True)))
+    left_gram(b["pl_all"], left_scale * left_scale, 0, 4)
     g_tile.step1()
     next(scatter)
     g_tile.step2()
+    left_gram(b["pl_all"], left_scale * left_scale, 4, 5)
     next(scatter)
     g_tile.step3()
+    left_gram(b["pl_all"], left_scale * left_scale, 5, 6)
     for _ in scatter:
         pass
     g_tile.finish()
     norm = jnp.sum(b["tiles"][...], keepdims=True) / 1024.0
     scale = math.sqrt(FF) / (4.0 * jnp.sqrt(norm))
     b["a_b"][...] = (b["a"][...] * (scale * scale)).astype(BF)
-    g_a = ShardGather(net, b["a_b"], b["a_cols"])
+    g_a = ShardGather(net, b["a_b"], b["a_cols"], slots=g_right.slots.again())
     begin(g_a)
-
+    for j in range(3):
+        cut = pl.ds(j * 256, 256)
+        v = b["pl_all"][cut, :]
+        b["wl"][cut, :] = (left_scale * (1.5 * v.astype(F32) - 0.5 * dot(v, b["gl"][...]))).astype(BF)
+    mine = left_scale * (1.5 * b["pl_own"][...] - 0.5 * dot(b["pl_b"][...], b["gl"][...]))
+    g_a.step1()
+    left_gram(b["wl"], 1.0, 0, 5)
+    g_a.step2()
+    left_gram(b["wl"], 1.0, 5, 6)
+    new_bl[...] = math.sqrt(D) * (1.5 * mine - 0.5 * dot(mine.astype(BF), b["gl"][...]))
+    stores[5].start()
+    g_a.step3()
+    g_dir = ShardGather(net, b["dir_b"], b["dir_cols"], slots=g_left.slots.again())
+    begin(g_dir)
+    g_a.finish()
+
+    def mix(rows, factor, add, out, all_rows, before):
+        v = dot(b[rows][...], b["a_cols"][...])
+        b[out][...] = ((factor * v if factor != 1.0 else v) + add * b["p"][...]).astype(BF)
+        g = TensorGather(net, b[out], b[all_rows], slots=before.slots.again())
+        begin(g)
+        return g
+
+    t_y = mix("p_rows", 0.0625, -0.5625, "y1_b", "y1_rows", t_stat)
+    g_dir.step1()
+    t_y.step1()
+    g_dir.step2()
+    t_y.step2()
+    g_dir.step3()
+    t_y.finish()
+    t_y = mix("y1_rows", 1.0, 1.6875, "y2_b", "y2_rows", t_power)
+    t_y.step1()
     g_dir.finish()
-    g_pl.finish()
-    pl_swap = swap(b["pl_all"])
     back = dot(b["lq"][...], b["dir_cols"][...]).astype(BF)
     for j in range(8):
         b["upart"][j % 2, j // 2] = dot_nt(back, b["qcols"][pl.ds(j * COLS, COLS), :]).astype(BF)
     to_update = line_scatter(net, b["upart"], update, b["u0"], b["uq"], b["u1"], b["u2"])
     next(to_update)
-    g_a.step1()
-    next(to_update)
-
-    pl_swap.recv()
-
-    def left_squares(j, total):
-        v = b["pl_all"][pl.ds(pl.multiple_of(j * 16, 16), 16), :].astype(F32)
-        return total + jnp.sum(v * v, axis=0, keepdims=True)
-
-    left_total = lax.fori_loop(0, D // 16, left_squares, jnp.zeros((1, D), F32))
-    left_scale = math.sqrt(D) / (4.0 * jnp.sqrt(jnp.sum(left_total, keepdims=True)))
-
-    def left_gram(ref, factor, lo, hi):
-        for j in range(lo, hi):
-            cut = pl.ds(j * 128, 128)
-            b["gl"][cut, :] = (dot_tn(ref[:, cut], ref[...]) * factor).astype(BF)
-
-    left_gram(b["pl_all"], left_scale * left_scale, 0, 6)
-    g_a.step2()
-    next(to_update)
-    g_a.step3()
-    g_a.finish()
-
-    def mix(rows, factor, add, out, all_rows):
-        v = dot(b[rows][...], b["a_cols"][...])
-        b[out][...] = ((factor * v if factor != 1.0 else v) + add * b["p"][...]).astype(BF)
-        g = TensorGather(net, b[out], b[all_rows])
-        begin(g)
-        return g
-
-    t_y = mix("p_rows", 0.0625, -0.5625, "y1_b", "y1_rows")
-    for _ in to_update:
-        pass
-    t_y.step1()
-    for j in range(3):
-        cut = pl.ds(j * 256, 256)
-        v = b["pl_all"][cut, :]
-        b["wl"][cut, :] = (left_scale * (1.5 * v.astype(F32) - 0.5 * dot(v, b["gl"][...]))).astype(BF)
-    mine = left_scale * (1.5 * b["pl_own"][...] - 0.5 * dot(b["pl_b"][...], b["gl"][...]))
-    b["pl_own"][...] = mine
     t_y.step2()
     t_y.finish()
-    t_y = mix("y1_rows", 1.0, 1.6875, "y2_b", "y2_rows")
-    left_gram(b["wl"], 1.0, 0, 3)
+    t_y = mix("y2_rows", 1.0, -2.4375, "y3_b", "y3_rows", t_stat)
+    next(to_update)
     t_y.step1()
-    left_gram(b["wl"], 1.0, 3, 6)
-    t_y.step2()
-    t_y.finish()
-    t_y = mix("y2_rows", 1.0, -2.4375, "y3_b", "y3_rows")
-    mine = b["pl_own"][...]
-    new_bl[...] = math.sqrt(D) * (1.5 * mine - 0.5 * dot(mine.astype(BF), b["gl"][...]))
-    t_y.step1()
+    next(to_update)
     t_y.step2()
     t_y.finish()
     v = dot(b["y3_rows"][...], b["a_cols"][...])
     new_br[...] = (math.sqrt(FF) * scale) * (2.25 * b["p"][...] + v)
-    assert net.count <= SEMS and locals_used[0] <= 16
+    stores[6].start()
+    for _ in to_update:
+        pass
+    stores[0].start()
+    assert net.taken <= SEMS and locals_used[0] <= 16
     cast.drain()
     net.drain()
+    for store in stores:
+        store.wait()
 
 
 def emit(*refs):
-    for a, o in zip(refs[:7], refs[7:]):
-        o[...] = a[...]
+    held, sem = refs[14:21], refs[21]
+    into = [pltpu.make_async_copy(refs[k], held[k], sem.at[0, k]) for k in range(7)]
+    onto = [pltpu.make_async_copy(held[k], refs[7 + k], sem.at[1, k]) for k in range(7)]
+    for copy in into:
+        copy.start()
+    for copy, store in zip(into, onto):
+        copy.wait()
+        store.start()
+    for store in onto:
+        store.wait()
 
 
 def local(gradient, moment_one, moment_two, stat_left, stat_right, basis_left, basis_right):
     args = (gradient, moment_one, moment_two, stat_left, stat_right, basis_left, basis_right)
-    vm = pl.BlockSpec(memory_space=pltpu.VMEM)
     out = pl.pallas_call(
         kernel,
         out_shape=[jax.ShapeDtypeStruct(a.shape, a.dtype) for a in args],
         in_specs=[pl.BlockSpec(memory_space=pl.ANY)] * 7,
-        out_specs=[vm] * 7,
+        out_specs=[pl.BlockSpec(memory_space=pl.ANY)] * 7,
         scratch_shapes=[pltpu.VMEM(shape, dtype) for shape, dtype in BUFFERS.values()]
         + [
+            pltpu.SemaphoreType.DMA((POOL + 8,)),
             pltpu.SemaphoreType.DMA((SEMS,)),
-            pltpu.SemaphoreType.DMA((SEMS,)),
-            pltpu.SemaphoreType.DMA((23,)),
+            pltpu.SemaphoreType.DMA((30,)),
         ]
-        + [pltpu.VMEM(a.shape, a.dtype) for a in args],
+        + [pltpu.VMEM(a.shape, a.dtype) for a in args * 2],
         compiler_params=pltpu.CompilerParams(
             collective_id=0, has_side_effects=True, vmem_limit_bytes=63 * 2**20
         ),
         name="step",
     )(*args)
+    hbm = pl.BlockSpec(memory_space=pl.ANY)
     return pl.pallas_call(
         emit,
         out_shape=[jax.ShapeDtypeStruct(a.shape, a.dtype) for a in args],
-        in_specs=[vm] * 7,
-        out_specs=[vm] * 7,
+        in_specs=[hbm] * 7,
+        out_specs=[hbm] * 7,
+        scratch_shapes=[pltpu.VMEM(a.shape, a.dtype) for a in args] + [pltpu.SemaphoreType.DMA((2, 7))],
         compiler_params=pltpu.CompilerParams(vmem_limit_bytes=63 * 2**20),
         name="emit",
     )(*out)

time: 135 us -> 125 us (0.926)
  Pallas kernels: 132 us -> 122 us
    pallas_call x1, Pallas kernels: 130 us -> 120 us  [local(): pl.pallas_call(kernel, out_shape=[jax.ShapeDtypeStruct(a.shape, a.dtype)...]
where the time goes in v4:
time: 125 us; the launch traced here: 123 us
  Pallas kernels  122 us (98%)
    pallas_call x1, Pallas kernels, local(): pl.pallas_call(kernel, out_shape=[jax.ShapeDtypeStruct(a.shape, a.dtype)...  120 us

profile of v4, /device:TPU:0, one launch (start us, length us, event | category | flops | bytes accessed | tf_op | source)
XLA Modules:
  0.0 123.0 jit_solution(1843504011828575075)
XLA Ops:
  0.6 120.1 %step.1 = (bf16[48,384]{1,0:T(8,128)(2,1)}, f32[48,384]{1,0:T(8,128)}, f32[48,384]{1,0:T(8,128)}, f32[48,768]{1,0:T(8,128)}, f32[192,384]{1,0:T(8,128)}, /*index=5*/f32[48,768]{1,0:T(8,128)}, f32[192,384]{1,0:T(8,128)}) custom-call(bf16[48,384]{1,0:T(8,128)(2,1)} %refs_0_.1, f32[48,384]{1,0:T(8,128)} %refs_1_.1, f32[48,384]{1,0:T(8,128)} %refs_2_.1, ...), custom_call_target="tpu_custom_call" | custom-call | tf_op jit(solution)/shard_map/step/pallas_call | solution.py:758
  120.7 2.1 %emit.1 = (bf16[48,384]{1,0:T(8,128)(2,1)}, f32[48,384]{1,0:T(8,128)}, f32[48,384]{1,0:T(8,128)}, f32[48,768]{1,0:T(8,128)}, f32[192,384]{1,0:T(8,128)}, /*index=5*/f32[48,768]{1,0:T(8,128)}, f32[192,384]{1,0:T(8,128)}) custom-call(bf16[48,384]{1,0:T(8,128)(2,1)} %get-tuple-element.14.refs_0_, f32[48,384]{1,0:T(8,128)} %get-tuple-element.15.refs_1_, ...), custom_call_target="tpu_custom_call" | custom-call | tf_op jit(solution)/shard_map/emit/pallas_call | solution.py:776

commit v5 on v4

--- a/solution.py
+++ b/solution.py
@@ -139,16 +139,17 @@
         if key in self.m:
             self.m[key].recv()
 
-    def start(self):
+    def start(self, only=(0, 1)):
         n = self.net
-        for i, (lo, mid, hi) in self.flows:
+        flows = [f for f in self.flows if f[0] in only]
+        for i, (lo, mid, hi) in flows:
             for sgn in (1, -1):
                 self.go(i, 0, sgn, 0, 0, lo, hi, (i, "a", sgn), own=True)
             if self.direct:
                 src = self.src.at[pl.ds(lo, hi - lo), :]
                 landing = self.view(self.rel(i, 2, 0), lo, hi)
                 self.m[i, "aa", 1] = n.send(src, self.view((0, 0), lo, hi), landing, "2" + self.axes(i)[0], self.slots)
-        for i, (lo, mid, hi) in self.flows:
+        for i, (lo, mid, hi) in flows:
             for sgn in (1, -1):
                 self.go(i, 1, sgn, 0, 0, lo, hi, (i, "b", 0, sgn), own=True)
 
@@ -421,7 +422,8 @@
         r.middle()
     yield
     for i, r in enumerate(later):
-        out[pl.ds(i * h, h), :] = r.total()
+        out[pl.ds(i * h, h), :] = r.total().astype(out.dtype)
+        yield
 
 
 def line_scatter(net, part, out, g0, q, g1, g2):
@@ -460,7 +462,7 @@
     return lax.dot_general(a, b, (((1,), (1,)), ((), ())), preferred_element_type=F32)
 
 
-SEMS, POOL = 268, 72
+SEMS, POOL = 208, 56
 ROWS, COLS, LROWS = FF // 16, FF // 8, D // 16
 BUFFERS = dict(
     lq=((LROWS, D), BF),
@@ -494,7 +496,6 @@
     fq=((2, 4, ROWS // 2, COLS), BF),
     fg1=((2, 2, ROWS // 4, COLS), BF),
     fg2=((2, 2, ROWS // 2, COLS), BF),
-    a=((ROWS, COLS), F32),
     a_b=((ROWS, COLS), BF),
     a_cols=((FF, COLS), BF),
     y1_b=((ROWS, COLS), BF),
@@ -573,9 +574,9 @@
     begin(t_lterms)
     g_right.step1()
     cast.middle()
+    g_right.step2()
     g_left.step3()
     t_lterms.step1()
-    g_right.step2()
     cast.finish()
 
     new_sr[...] = beta * stat_r[...] + ((1.0 - beta) / D) * dot_tn(b["gs"][...], gcols[...])
@@ -583,11 +584,11 @@
     t_stat = TensorGather(net, b["s_b"], b["s_rows"])
     begin(t_stat)
     stores[4].start()
-    g_left.finish()
-    left_swap = swap(b["lall"])
     t_lterms.step2()
     g_right.step3()
     t_stat.step1()
+    g_left.finish()
+    left_swap = swap(b["lall"])
     left_swap.recv()
     t_lterms.finish()
     gram = b["lparts"][pl.ds(0, LROWS), :].astype(F32)
@@ -596,7 +597,9 @@
     new_sl[...] = beta * stat_l[...] + ((1.0 - beta) / FF) * gram
     b["pl_own"][...] = dot(new_sl[...].astype(BF), b["lall"][...])
     b["pl_b"][...] = b["pl_own"][...].astype(BF)
-    g_pl = ShardGather(net, b["pl_b"].at[:, lanes(net.c)], b["pl_all"].at[:, lanes(net.c)])
+    g_pl = ShardGather(
+        net, b["pl_b"].at[:, lanes(net.c)], b["pl_all"].at[:, lanes(net.c)], slots=g_grad.slots.again()
+    )
     begin(g_pl)
     stores[3].start()
     b["half_all"][...] = dot_tn(b["lall"][...], gcols[...]).astype(BF)
@@ -623,7 +626,7 @@
         v = dot_tn(b["p_rows"][:, pl.ds(pl.multiple_of(zt * D, 128), D)], b["p_b"][...]).astype(BF)
         b["part"][zt] = v.reshape(4, ROWS, COLS)
 
-    scatter = plane_scatter(net, b["part"], b["a"], b["f1"], b["f2"], b["fq"], b["fg1"], b["fg2"])
+    scatter = plane_scatter(net, b["part"], b["a_b"], b["f1"], b["f2"], b["fq"], b["fg1"], b["fg2"])
     term(2)
     next(scatter)
     term(1)
@@ -638,7 +641,7 @@
 
     total = lax.fori_loop(0, ROWS // 16, squares, jnp.zeros((1, FF), F32))
     b["tile"][...] = jnp.broadcast_to(jnp.sum(total, keepdims=True), (8, 128))
-    g_tile = ShardGather(net, b["tile"], b["tiles"])
+    g_tile = ShardGather(net, b["tile"], b["tiles"], slots=g_left.slots.again())
     begin(g_tile)
     t_half.finish()
     rot = dot(b["half_rows"][...], b["qcols"][...])
@@ -673,14 +676,13 @@
     next(scatter)
     g_tile.step3()
     left_gram(b["pl_all"], left_scale * left_scale, 5, 6)
-    for _ in scatter:
-        pass
-    g_tile.finish()
-    norm = jnp.sum(b["tiles"][...], keepdims=True) / 1024.0
-    scale = math.sqrt(FF) / (4.0 * jnp.sqrt(norm))
-    b["a_b"][...] = (b["a"][...] * (scale * scale)).astype(BF)
     g_a = ShardGather(net, b["a_b"], b["a_cols"], slots=g_right.slots.again())
-    begin(g_a)
+    next(scatter)
+    g_a.start((0,))
+    next(scatter)
+    g_a.start((1,))
+    g_a.local(lsem.at[locals_used[0]])
+    locals_used[0] += 1
     for j in range(3):
         cut = pl.ds(j * 256, 256)
         v = b["pl_all"][cut, :]
@@ -693,25 +695,29 @@
     new_bl[...] = math.sqrt(D) * (1.5 * mine - 0.5 * dot(mine.astype(BF), b["gl"][...]))
     stores[5].start()
     g_a.step3()
-    g_dir = ShardGather(net, b["dir_b"], b["dir_cols"], slots=g_left.slots.again())
+    g_dir = ShardGather(net, b["dir_b"], b["dir_cols"], slots=g_grad.slots.again())
     begin(g_dir)
+    g_tile.finish()
+    norm = jnp.sum(b["tiles"][...], keepdims=True) / 1024.0
+    scale = math.sqrt(FF) / (4.0 * jnp.sqrt(norm))
+    square = scale * scale
     g_a.finish()
 
     def mix(rows, factor, add, out, all_rows, before):
         v = dot(b[rows][...], b["a_cols"][...])
-        b[out][...] = ((factor * v if factor != 1.0 else v) + add * b["p"][...]).astype(BF)
+        b[out][...] = (factor * v + add * b["p"][...]).astype(BF)
         g = TensorGather(net, b[out], b[all_rows], slots=before.slots.again())
         begin(g)
         return g
 
-    t_y = mix("p_rows", 0.0625, -0.5625, "y1_b", "y1_rows", t_stat)
+    t_y = mix("p_rows", 0.0625 * square, -0.5625, "y1_b", "y1_rows", t_stat)
     g_dir.step1()
     t_y.step1()
     g_dir.step2()
     t_y.step2()
     g_dir.step3()
     t_y.finish()
-    t_y = mix("y1_rows", 1.0, 1.6875, "y2_b", "y2_rows", t_power)
+    t_y = mix("y1_rows", square, 1.6875, "y2_b", "y2_rows", t_power)
     t_y.step1()
     g_dir.finish()
     back = dot(b["lq"][...], b["dir_cols"][...]).astype(BF)
@@ -721,14 +727,14 @@
     next(to_update)
     t_y.step2()
     t_y.finish()
-    t_y = mix("y2_rows", 1.0, -2.4375, "y3_b", "y3_rows", t_stat)
+    t_y = mix("y2_rows", square, -2.4375, "y3_b", "y3_rows", t_stat)
     next(to_update)
     t_y.step1()
     next(to_update)
     t_y.step2()
     t_y.finish()
     v = dot(b["y3_rows"][...], b["a_cols"][...])
-    new_br[...] = (math.sqrt(FF) * scale) * (2.25 * b["p"][...] + v)
+    new_br[...] = (math.sqrt(FF) * scale) * (2.25 * b["p"][...] + square * v)
     stores[6].start()
     for _ in to_update:
         pass

time: 125 us -> 123 us (0.984)
  no operation moved by 1% of the time
where the time goes in v5:
time: 123 us; the launch traced here: 122 us
  Pallas kernels  121 us (98%)
    pallas_call x1, Pallas kernels, local(): pl.pallas_call(kernel, out_shape=[jax.ShapeDtypeStruct(a.shape, a.dtype)...  119 us

profile of v5, /device:TPU:0, one launch (start us, length us, event | category | flops | bytes accessed | tf_op | source)
XLA Modules:
  0.0 122.2 jit_solution(5828809628111544089)
XLA Ops:
  0.6 119.3 %step.1 = (bf16[48,384]{1,0:T(8,128)(2,1)}, f32[48,384]{1,0:T(8,128)}, f32[48,384]{1,0:T(8,128)}, f32[48,768]{1,0:T(8,128)}, f32[192,384]{1,0:T(8,128)}, /*index=5*/f32[48,768]{1,0:T(8,128)}, f32[192,384]{1,0:T(8,128)}) custom-call(bf16[48,384]{1,0:T(8,128)(2,1)} %refs_0_.1, f32[48,384]{1,0:T(8,128)} %refs_1_.1, f32[48,384]{1,0:T(8,128)} %refs_2_.1, ...), custom_call_target="tpu_custom_call" | custom-call | tf_op jit(solution)/shard_map/step/pallas_call | solution.py:764
  119.9 2.1 %emit.1 = (bf16[48,384]{1,0:T(8,128)(2,1)}, f32[48,384]{1,0:T(8,128)}, f32[48,384]{1,0:T(8,128)}, f32[48,768]{1,0:T(8,128)}, f32[192,384]{1,0:T(8,128)}, /*index=5*/f32[48,768]{1,0:T(8,128)}, f32[192,384]{1,0:T(8,128)}) custom-call(bf16[48,384]{1,0:T(8,128)(2,1)} %get-tuple-element.14.refs_0_, f32[48,384]{1,0:T(8,128)} %get-tuple-element.15.refs_1_, ...), custom_call_target="tpu_custom_call" | custom-call | tf_op jit(solution)/shard_map/emit/pallas_call | solution.py:782

commit v6 on v5

--- a/solution.py
+++ b/solution.py
@@ -696,7 +696,6 @@
     stores[5].start()
     g_a.step3()
     g_dir = ShardGather(net, b["dir_b"], b["dir_cols"], slots=g_grad.slots.again())
-    begin(g_dir)
     g_tile.finish()
     norm = jnp.sum(b["tiles"][...], keepdims=True) / 1024.0
     scale = math.sqrt(FF) / (4.0 * jnp.sqrt(norm))
@@ -711,13 +710,14 @@
         return g
 
     t_y = mix("p_rows", 0.0625 * square, -0.5625, "y1_b", "y1_rows", t_stat)
+    begin(g_dir)
+    t_y.step1()
     g_dir.step1()
-    t_y.step1()
+    t_y.step2()
     g_dir.step2()
-    t_y.step2()
-    g_dir.step3()
     t_y.finish()
     t_y = mix("y1_rows", square, 1.6875, "y2_b", "y2_rows", t_power)
+    g_dir.step3()
     t_y.step1()
     g_dir.finish()
     back = dot(b["lq"][...], b["dir_cols"][...]).astype(BF)

time: 123 us -> 123 us (level)
  no operation moved by 1% of the time
where the time goes in v6:
time: 123 us; the launch traced here: 122 us
  Pallas kernels  121 us (98%)
    pallas_call x1, Pallas kernels, local(): pl.pallas_call(kernel, out_shape=[jax.ShapeDtypeStruct(a.shape, a.dtype)...  119 us

profile of v6, /device:TPU:0, one launch (start us, length us, event | category | flops | bytes accessed | tf_op | source)
XLA Modules:
  0.0 122.1 jit_solution(15807675753384003229)
XLA Ops:
  0.6 119.2 %step.1 = (bf16[48,384]{1,0:T(8,128)(2,1)}, f32[48,384]{1,0:T(8,128)}, f32[48,384]{1,0:T(8,128)}, f32[48,768]{1,0:T(8,128)}, f32[192,384]{1,0:T(8,128)}, /*index=5*/f32[48,768]{1,0:T(8,128)}, f32[192,384]{1,0:T(8,128)}) custom-call(bf16[48,384]{1,0:T(8,128)(2,1)} %refs_0_.1, f32[48,384]{1,0:T(8,128)} %refs_1_.1, f32[48,384]{1,0:T(8,128)} %refs_2_.1, ...), custom_call_target="tpu_custom_call" | custom-call | tf_op jit(solution)/shard_map/step/pallas_call | solution.py:764
  119.9 2.1 %emit.1 = (bf16[48,384]{1,0:T(8,128)(2,1)}, f32[48,384]{1,0:T(8,128)}, f32[48,384]{1,0:T(8,128)}, f32[48,768]{1,0:T(8,128)}, f32[192,384]{1,0:T(8,128)}, /*index=5*/f32[48,768]{1,0:T(8,128)}, f32[192,384]{1,0:T(8,128)}) custom-call(bf16[48,384]{1,0:T(8,128)(2,1)} %get-tuple-element.14.refs_0_, f32[48,384]{1,0:T(8,128)} %get-tuple-element.15.refs_1_, ...), custom_call_target="tpu_custom_call" | custom-call | tf_op jit(solution)/shard_map/emit/pallas_call | solution.py:782

commit v7 on v6

--- a/solution.py
+++ b/solution.py
@@ -462,7 +462,7 @@
     return lax.dot_general(a, b, (((1,), (1,)), ((), ())), preferred_element_type=F32)
 
 
-SEMS, POOL = 208, 56
+SEMS, POOL = 208, 40
 ROWS, COLS, LROWS = FF // 16, FF // 8, D // 16
 BUFFERS = dict(
     lq=((LROWS, D), BF),

time: 123 us -> 123 us (level)
  no operation moved by 1% of the time
where the time goes in v7:
time: 123 us; the launch traced here: 122 us
  Pallas kernels  121 us (98%)
    pallas_call x1, Pallas kernels, local(): pl.pallas_call(kernel, out_shape=[jax.ShapeDtypeStruct(a.shape, a.dtype)...  119 us

profile of v7, /device:TPU:0, one launch (start us, length us, event | category | flops | bytes accessed | tf_op | source)
XLA Modules:
  0.0 122.0 jit_solution(8216570195231511023)
XLA Ops:
  0.6 119.1 %step.1 = (bf16[48,384]{1,0:T(8,128)(2,1)}, f32[48,384]{1,0:T(8,128)}, f32[48,384]{1,0:T(8,128)}, f32[48,768]{1,0:T(8,128)}, f32[192,384]{1,0:T(8,128)}, /*index=5*/f32[48,768]{1,0:T(8,128)}, f32[192,384]{1,0:T(8,128)}) custom-call(bf16[48,384]{1,0:T(8,128)(2,1)} %refs_0_.1, f32[48,384]{1,0:T(8,128)} %refs_1_.1, f32[48,384]{1,0:T(8,128)} %refs_2_.1, ...), custom_call_target="tpu_custom_call" | custom-call | tf_op jit(solution)/shard_map/step/pallas_call | solution.py:764
  119.7 2.1 %emit.1 = (bf16[48,384]{1,0:T(8,128)(2,1)}, f32[48,384]{1,0:T(8,128)}, f32[48,384]{1,0:T(8,128)}, f32[48,768]{1,0:T(8,128)}, f32[192,384]{1,0:T(8,128)}, /*index=5*/f32[48,768]{1,0:T(8,128)}, f32[192,384]{1,0:T(8,128)}) custom-call(bf16[48,384]{1,0:T(8,128)(2,1)} %get-tuple-element.14.refs_0_, f32[48,384]{1,0:T(8,128)} %get-tuple-element.15.refs_1_, ...), custom_call_target="tpu_custom_call" | custom-call | tf_op jit(solution)/shard_map/emit/pallas_call | solution.py:782
